TPU v7x, 256 devices: a whole 4x4x8 slice. The times are simulated.
256 devices in a mesh: gx: 8 (over x, core), gy: 8 (over z), cyc: 4 (over y).
Axes of the slice: x: 4, y: 4, z: 8, core: 2. Of those that a mesh axis runs over, the one named last changes fastest.
Arguments:
- displacement: bfloat16 [2, 192, 1024, 1024], P(None, 'gx', 'gy', 'cyc'), may hold values from -6 to 6
Outputs:
- basis: float32 [2, 192, 1024, 128], P(None, 'gx', 'gy', 'cyc')
All inputs are finite; a program needn't handle non-finite values.
Results may differ from a plain program's by a relative error of at most 0.0003.
Values may be sent and summed in bfloat16 or wider, within the bound.
No kernel may reach another device: no remote copies, remote signals or barrier semaphores. Data moves between devices by JAX's collectives and lax.ppermute only.
A program may use at most 128 MiB of HBM per device.

v0:
```python
import jax
import jax.numpy as jnp
from jax import lax
from jax.experimental import pallas as pl
from jax.experimental.pallas import tpu as pltpu
from jax.sharding import PartitionSpec as P

RANK = 128
F32 = jnp.float32
BF = jnp.bfloat16
HIGH = lax.Precision.HIGHEST
ROWS = 4
LIMIT = 56 * 2**20


def mm(a, b, ca, cb):
    return lax.dot_general(
        a, b, (((ca,), (cb,)), ((), ())), precision=HIGH, preferred_element_type=F32
    )


def fast(a, b, ca, cb):
    return lax.dot_general(a, b, (((ca,), (cb,)), ((), ())), preferred_element_type=F32)


def thirds(v):
    top = v.astype(BF).astype(F32)
    rest = v - top
    mid = rest.astype(BF).astype(F32)
    return top, mid, rest - mid


def small_inverse(entry, n):
    d = [row[:] for row in entry]
    l = [[None] * n for _ in range(n)]
    r = [None] * n
    for j in range(n):
        g = lax.rsqrt(d[j][j])
        g = g * (1.5 - (0.5 * d[j][j]) * (g * g))
        r[j] = g
        for i in range(j + 1, n):
            l[i][j] = d[i][j] * g
        for k in range(j + 1, n):
            for i in range(k, n):
                d[i][k] = d[i][k] - l[i][j] * l[k][j]
    x = [[None] * n for _ in range(n)]
    for j in range(n):
        x[j][j] = r[j]
        for i in range(j + 1, n):
            t = l[i][j] * x[j][j]
            for k in range(j + 1, i):
                t = t + l[i][k] * x[k][j]
            x[i][j] = -(t * r[i])
    return x


def inverse_factor(work, n):
    step = 8
    sub = lax.broadcasted_iota(jnp.int32, (step, n), 0)
    for at in range(0, n, step):
        rows = work[at : at + step, :]
        block = rows[:, at : at + step]
        entry = [
            [jnp.broadcast_to(block[i : i + 1, j : j + 1], (step, n)) for j in range(i + 1)]
            for i in range(step)
        ]
        x = small_inverse(entry, step)
        left = jnp.zeros((step, n), F32)
        right = jnp.zeros((step, n), F32)
        for j in range(step):
            col = x[j][j]
            for i in range(j + 1, step):
                col = jnp.where(sub >= i, x[i][j], col)
            col = jnp.where(sub < j, 0.0, col)
            left = left + col * jnp.broadcast_to(rows[j : j + 1, :n], (step, n))
            right = right + col * jnp.broadcast_to(rows[j : j + 1, n:], (step, n))
        new = jnp.concatenate([left, right], axis=1)
        work[at : at + step, :] = new
        if at + step < n:
            a, b, c = thirds(new)
            lhs = jnp.concatenate([a, a, a, b, b, c], axis=0)[:, :n].astype(BF)
            rhs = jnp.concatenate([a, b, c, a, b, a], axis=0).astype(BF)
            prod = fast(lhs, rhs, 0, 0)
            work[at + step :, :] = work[at + step :, :] - prod[at + step :, :]


def eye(n):
    row = lax.broadcasted_iota(jnp.int32, (n, n), 0)
    return (row == lax.broadcasted_iota(jnp.int32, (n, n), 1)).astype(F32)


def vectors_of(h, work, moved, found):
    w = h.shape[0]
    n = w // 2
    identity = eye(n)
    trace = jnp.sum(h[:n, :n] * identity) + jnp.sum(h[n:, n:] * identity)
    hn = h * (1.0 / (trace / w + 1e-06))
    moved[...] = mm(hn, hn[:, :n] + hn[:, n:], 1, 0)

    def turn(at, carry):
        z = moved[...]
        gram = mm(z, z, 0, 0)
        shift = jnp.where(at == 0, 4e-7, 0.0)
        work[:, :n] = gram + identity * (jnp.sum(gram * identity) * shift)
        work[:, n:] = identity
        inverse_factor(work, n)
        v = mm(z, work[:, n:], 1, 1)
        found[...] = v
        moved[...] = mm(hn, v, 1, 0)
        return carry

    lax.fori_loop(0, 2, turn, 0)
    return found[...]


def first_kernel(g_ref, out_ref, work, moved, found):
    h = joined_gram(g_ref[:RANK], g_ref[RANK : 2 * RANK], g_ref[2 * RANK :])
    w = h.shape[0]
    v = vectors_of(h, work, moved, found)
    out_ref[:w] = v
    out_ref[w:] = mm(v, mm(h, v, 1, 0), 0, 0)


def scratch():
    return [
        pltpu.VMEM((RANK, 2 * RANK), F32),
        pltpu.VMEM((2 * RANK, RANK), F32),
        pltpu.VMEM((2 * RANK, RANK), F32),
    ]


def first_level(gram):
    return pl.pallas_call(
        first_kernel,
        out_shape=jax.ShapeDtypeStruct((3 * RANK, RANK), F32),
        scratch_shapes=scratch(),
    )(gram)


def joined_gram(own_gram, cross, far_gram):
    top = jnp.concatenate([own_gram, cross], axis=1)
    low = jnp.concatenate([cross.T, far_gram], axis=1)
    return jnp.concatenate([top, low], axis=0)


def level_kernel(own_ref, cross_ref, far_ref, out_ref, work, moved, found):
    w = own_ref.shape[0] - RANK
    h = joined_gram(own_ref[w:], cross_ref[...], far_ref[w:])
    u = vectors_of(h, work, moved, found)
    out_ref[:w] = mm(own_ref[:w], u[:RANK], 1, 0)
    out_ref[w : 2 * w] = mm(far_ref[:w], u[RANK:], 1, 0)
    out_ref[2 * w :] = mm(u, mm(h, u, 1, 0), 0, 0)


def next_level(own, cross, far):
    w = own.shape[0] - RANK
    return pl.pallas_call(
        level_kernel,
        out_shape=jax.ShapeDtypeStruct((2 * w + RANK, RANK), F32),
        scratch_shapes=scratch(),
    )(own, cross, far)


def last_kernel(own_ref, cross_ref, far_ref, pick_ref, out_ref, work, moved, found):
    w = own_ref.shape[0] - RANK
    h = joined_gram(own_ref[w:], cross_ref[...], far_ref[w:])
    u = vectors_of(h, work, moved, found)
    share = pick_ref.shape[0]
    for at, ref in ((0, own_ref), (1, far_ref)):
        mine = mm(pick_ref[...], u[at * RANK : (at + 1) * RANK], 1, 1)
        part = mm(mine, ref[:w], 1, 1)
        top = part.astype(BF)
        out_ref[:share, at * w : (at + 1) * w] = top
        out_ref[share:, at * w : (at + 1) * w] = (part - top.astype(F32)).astype(BF)


def last_level(own, cross, far, pick):
    w = own.shape[0] - RANK
    return pl.pallas_call(
        last_kernel,
        out_shape=jax.ShapeDtypeStruct((2 * pick.shape[0], 2 * w), BF),
        scratch_shapes=scratch(),
    )(own, cross, far, pick)


def project_kernel(own_ref, far_ref, *refs):
    *blocks, o_ref = refs
    w = own_ref.shape[0] - RANK
    own = own_ref[:w]
    total = jnp.zeros(o_ref.shape, F32)
    for g, block in enumerate(blocks):
        snaps = block.shape[0]
        seen = mm(block[...], own, 1, 0)
        total += mm(seen, far_ref[g * snaps : (g + 1) * snaps], 0, 0)
    o_ref[...] = total


def project(own, far, blocks):
    return pl.pallas_call(project_kernel, out_shape=jax.ShapeDtypeStruct((RANK, RANK), F32))(
        own, far, *blocks
    )


def feature_kernel(count, u_ref, halo_ref, *refs):
    left = refs[: 2 * count]
    hi_ref, lo_ref, gram_ref, field, sides, sums = refs[2 * count :]
    at = pl.program_id(0)
    _, height, wide, snaps = u_ref.shape

    @pl.when(at == 0)
    def _():
        sides[...] = halo_ref[:, :, wide:, :].astype(F32)
        field[:, 0] = halo_ref[:, 0, :wide, :].astype(F32)
        field[:, height + 1] = halo_ref[:, 1, :wide, :].astype(F32)
        field[:, 1] = u_ref[:, 0].astype(F32)
        sums[...] = jnp.zeros_like(sums)

    edge = lax.broadcasted_iota(jnp.int32, (wide, 128), 0)

    def one(r, carry):
        i = at * ROWS + r

        @pl.when(i + 1 < height)
        def _():
            field[:, i + 2] = u_ref[:, i + 1].astype(F32)

        for start in range(0, snaps, 128):
            lanes = slice(start, start + 128)

            def along_x(c):
                return field[c, i + 2, :, lanes] - field[c, i, :, lanes]

            def along_y(c):
                here = field[c, i + 1, :, lanes]
                back = jnp.where(
                    edge == 0, sides[c, 0, pl.ds(i, 1), :][:, lanes], pltpu.roll(here, 1, 0)
                )
                ahead = jnp.where(
                    edge == wide - 1,
                    sides[c, 1, pl.ds(i, 1), :][:, lanes],
                    pltpu.roll(here, wide - 1, 0),
                )
                return ahead - back

            strain_xx = along_x(0)
            strain_yy = along_y(1)
            shear = along_x(1) + along_y(0)
            values = (
                0.5 * (strain_xx + strain_yy),
                0.25 * (strain_xx * strain_yy) - 0.0625 * (shear * shear),
            )
            span = pl.ds(pl.multiple_of(r * wide, wide), wide)
            for k, value in enumerate(values):
                hi = value.astype(BF)
                hi_ref[k, span, lanes] = hi
                lo_ref[k, span, lanes] = (value - hi.astype(F32)).astype(BF)
        return carry

    lax.fori_loop(0, ROWS, one, 0)
    for k in range(2):
        hi = hi_ref[k]
        lo = lo_ref[k]
        if count == 0:
            sums[:, :snaps] += fast(hi, hi, 0, 0)
            sums[:, snaps:] += fast(hi, lo, 0, 0)
        for g in range(count):
            other = left[2 * g][k]
            rest = left[2 * g + 1][k]
            sums[:, g * snaps : (g + 1) * snaps] += (
                fast(hi, other, 0, 0) + fast(hi, rest, 0, 0) + fast(lo, other, 0, 0)
            )

    @pl.when(at == pl.num_programs(0) - 1)
    def _():
        if count == 0:
            mixed = sums[:, snaps:]
            total = sums[:, :snaps] + (mixed + mixed.T)
            gram_ref[:RANK] = total[:RANK, :RANK]
            gram_ref[RANK : 2 * RANK] = total[:RANK, RANK:]
            gram_ref[2 * RANK :] = total[RANK:, RANK:]
        else:
            gram_ref[...] = sums[:, : count * snaps]


def features(u, halo, lefts):
    _, height, wide, snaps = u.shape
    count = len(lefts)
    full = lambda array: pl.BlockSpec(array.shape, lambda i: (0,) * array.ndim)
    part = pl.BlockSpec((2, ROWS * wide, snaps), lambda i: (0, i, 0))
    half = jax.ShapeDtypeStruct((2, height * wide, snaps), BF)
    shape = (snaps, count * snaps) if count else (3 * RANK, RANK)
    hi, lo, gram = pl.pallas_call(
        lambda *refs: feature_kernel(count, *refs),
        grid=(height // ROWS,),
        in_specs=[full(u), full(halo)] + [part] * (2 * count),
        out_specs=(part, part, pl.BlockSpec(shape, lambda i: (0, 0))),
        out_shape=(half, half, jax.ShapeDtypeStruct(shape, F32)),
        scratch_shapes=[
            pltpu.VMEM((2, height + 2, wide, snaps), F32),
            pltpu.VMEM((2, 2, height, snaps), F32),
            pltpu.VMEM((snaps, max(count, 2) * snaps), F32),
        ],
        compiler_params=pltpu.CompilerParams(vmem_limit_bytes=LIMIT),
    )(u, halo, *[array for pair in lefts for array in pair])
    return (hi, lo), gram


def finish_kernel(*refs):
    *halves, w_ref, o_ref = refs
    groups = len(halves) // 2
    snaps = w_ref.shape[1] // groups
    share = w_ref.shape[0] // 2
    wide = o_ref.shape[-1]
    total = jnp.zeros((share, halves[0].shape[1]), F32)
    for g in range(groups):
        w = w_ref[:, g * snaps : (g + 1) * snaps]
        both = fast(w, halves[2 * g][0], 1, 1)
        total += both[:share] + both[share:]
        total += fast(w[:share], halves[2 * g + 1][0], 1, 1)
    for r in range(o_ref.shape[1]):
        o_ref[0, r] = total[:, r * wide : (r + 1) * wide]


def finish(pairs, weights, height, wide):
    rows = 8
    _, _, snaps = pairs[0][0].shape
    share = weights.shape[0] // 2
    part = pl.BlockSpec((1, rows * wide, snaps), lambda k, i: (k, i, 0))
    return pl.pallas_call(
        finish_kernel,
        grid=(2, height // rows),
        in_specs=[part] * (2 * len(pairs))
        + [pl.BlockSpec(weights.shape, lambda k, i: (0, 0))],
        out_specs=pl.BlockSpec((1, rows, share, wide), lambda k, i: (k, i, 0, 0)),
        out_shape=jax.ShapeDtypeStruct((2, height, share, wide), F32),
        compiler_params=pltpu.CompilerParams(vmem_limit_bytes=LIMIT),
    )(*[array for pair in pairs for array in pair], weights)


def edges(block, axis, dim):
    count = lax.axis_size(axis)
    forward = [(i, i + 1) for i in range(count - 1)]
    backward = [(target, source) for source, target in forward]
    low = lax.ppermute(
        lax.slice_in_dim(block, block.shape[dim] - 1, None, axis=dim), axis, forward
    )
    high = lax.ppermute(lax.slice_in_dim(block, 0, 1, axis=dim), axis, backward)
    return low, high


def halo_of(block):
    _, height, wide, snaps = block.shape
    x_low, x_high = edges(block, "gx", 1)
    y_low, y_high = edges(block, "gy", 2)
    low = jnp.concatenate([x_low[:, 0], y_low[:, :, 0]], axis=1)
    high = jnp.concatenate([x_high[:, 0], y_high[:, :, 0]], axis=1)
    return jnp.stack([low, high], axis=1)


def swapped(value, mask):
    pairs = [(source, source ^ mask) for source in range(lax.axis_size("cyc"))]
    return lax.ppermute(value, "cyc", pairs)


def scatter_sum(value, axis):
    count = lax.axis_size(axis)
    parts = lax.all_to_all(value, axis, 0, 0, tiled=True)
    return parts.reshape(count, -1, value.shape[1]).sum(0)


def gathered(value, axis):
    count = lax.axis_size(axis)
    copies = jnp.broadcast_to(value[None], (count,) + value.shape)
    return lax.all_to_all(copies.reshape(-1, value.shape[1]), axis, 0, 0, tiled=True)


def all_sum(value):
    flat = value.reshape(-1, 128)
    part = scatter_sum(flat, "gx")
    part = gathered(part, "gy").reshape(lax.axis_size("gy"), -1, 128).sum(0)
    return gathered(part, "gx").reshape(value.shape)


def on_device(displacement):
    _, height, wide, _ = displacement.shape
    groups = lax.axis_size("cyc")
    halo = halo_of(displacement)
    near = swapped(displacement, 1)
    side = swapped(displacement, 3)
    own, gram = features(displacement, halo, [])
    total = all_sum(gram)
    relayed, _ = lax.optimization_barrier((side, total))
    far = swapped(relayed, 1)
    level0 = first_level(total)
    pair, cross1 = features(near, swapped(halo, 1), [own])
    other0 = swapped(level0, 1)
    level1 = next_level(level0, all_sum(project(level0, other0, [cross1])), other0)
    fourth, cross3 = features(side, swapped(halo, 3), [own, pair])
    third, cross2 = features(far, swapped(halo, 2), [own, pair])
    other1 = swapped(level1, 2)
    share = RANK // groups
    column = lax.axis_index("cyc") * share + jnp.arange(share)
    pick = (column[:, None] == jnp.arange(RANK)[None, :]).astype(F32)
    total = all_sum(project(level1, other1, [cross2, cross3]))
    weights = last_level(level1, total, other1, pick)
    result = finish([own, pair, third, fourth], weights, height, wide)
    return result.transpose(0, 1, 3, 2)


def solution(mesh):
    return jax.shard_map(
        on_device,
        mesh=mesh,
        in_specs=(P(None, "gx", "gy", "cyc"),),
        out_specs=P(None, "gx", "gy", "cyc"),
        check_vma=False,
    )
```

profile of v0, /device:TPU:1, one launch (start us, length us, event | category | flops | bytes accessed | tf_op | source)
XLA Modules:
  0.0 371.9 jit_solution(8017990286174305)
XLA Ops:
  0.0 3.6 collective-permute-start.6
  3.6 1.0 slice_bitcast_fusion.1
  4.6 4.0 %collective-permute-start = (bf16[2,1,128,256]{3,2,0,1:T(8,128)(2,1)S(1)}, bf16[2,1,128,256]{3,2,0,1:T(8,128)(2,1)S(1)}, u32[]{:S(2)}, u32[]{:S(2)}) collective-permute-start(bf16[2,1,128,256]{3,2,0,1:T(8,128)(2,1)S(1)} %get-tuple-element.31), channel_id=1, source_target_pairs={{0,32},{32,64},{64,96},{96,128},{128,160},{160,192},{192,224},{1,3... | collective-permute-start | bytes 393224 | tf_op jit(solution)/shard_map/ppermute | solution.py:344
  8.5 1.1 fusion.1
  9.6 3.5 collective-permute-start.1
  13.2 1.9 collective-permute-start.2
  15.1 1.3 collective-permute-start.3
  16.5 0.0 collective-permute-done
  16.5 3.8 %collective-permute-done.3 = bf16[2,24,1,256]{3,1,0,2:T(8,128)(2,1)S(1)} collective-permute-done((bf16[2,24,1,256]{3,1,0,2:T(8,128)(2,1)S(1)}, bf16[2,24,1,256]{3,1,0,2:T(8,128)(2,1)S(1)}, u32[]{:S(2)}, u32[]{:S(2)}) %collective-permute-start.3) | collective-permute-done | bytes 24608 | tf_op jit(solution)/shard_map/ppermute | solution.py:347
  20.3 0.8 pad_maximum_fusion.refs_1_
  21.1 10.1 %shard_map.17 = (bf16[2,3072,256]{2,1,0:T(8,128)(2,1)}, bf16[2,3072,256]{2,1,0:T(8,128)(2,1)}, f32[384,128]{1,0:T(8,128)}) custom-call(bf16[2,24,128,256]{3,2,1,0:T(8,128)(2,1)} %refs_0_.1, bf16[2,2,152,256]{3,2,1,0:T(8,128)(2,1)} %pad_maximum_fusion.refs_1_), custom_call_target="tpu_custom_call" | custom-call | tf_op jit(solution)/shard_map/pallas_call | solution.py:292
  31.1 5.5 %all-to-all-start = ((f32[8,48,128]{2,1,0:T(8,128)}), f32[8,48,128]{2,1,0:T(8,128)}, u32[]{:S(2)}, u32[]{:S(2)}) async-start(f32[8,48,128]{2,1,0:T(8,128)} %bitcast.24), calls=%async_computation | async-start | bytes 393216 | tf_op jit(solution)/shard_map/all_to_all | solution.py:367
  36.6 6.0 %all-to-all-done = f32[8,48,128]{2,1,0:T(8,128)} async-done(((f32[8,48,128]{2,1,0:T(8,128)}), f32[8,48,128]{2,1,0:T(8,128)}, u32[]{:S(2)}, u32[]{:S(2)}) %all-to-all-start) | async-done | bytes 196640 | tf_op jit(solution)/shard_map/all_to_all | solution.py:367
  42.6 0.9 reduce_sum.54
  43.6 16.6 %all_to_all.69 = f32[8,48,128]{2,1,0:T(8,128)} all-to-all(f32[8,48,128]{2,1,0:T(8,128)S(1)} %broadcast_in_dim.12), channel_id=1, replica_groups=mesh['gx'=8,'gy'=8,'cyc'=4] {'gy'}, dimensions={0} | all-to-all | bytes 393216 | tf_op jit(solution)/shard_map/all_to_all | solution.py:374
  60.1 0.9 reduce_sum.55
  61.1 11.7 %all_to_all.70 = f32[8,48,128]{2,1,0:T(8,128)} all-to-all(f32[8,48,128]{2,1,0:T(8,128)S(1)} %broadcast_in_dim.13), channel_id=1, replica_groups=mesh['gx'=8,'gy'=8,'cyc'=4] {'gx'}, dimensions={0} | all-to-all | bytes 393216 | tf_op jit(solution)/shard_map/all_to_all | solution.py:374
  72.8 1.5 collective-permute-start.5
  74.3 18.1 %shard_map.21.own_ref = f32[384,128]{1,0:T(8,128)} custom-call(f32[384,128]{1,0:T(8,128)} %bitcast.19), custom_call_target="tpu_custom_call" | custom-call | tf_op jit(solution)/shard_map/pallas_call | solution.py:133
  92.4 0.1 collective-permute-start.10
  92.5 87.9 %collective-permute-done.5.refs_1_ = bf16[2,2,152,256]{3,2,1,0:T(8,128)(2,1)} collective-permute-done((bf16[2,2,152,256]{3,2,1,0:T(8,128)(2,1)S(1)}, bf16[2,2,152,256]{3,2,1,0:T(8,128)(2,1)}, u32[]{:S(2)}, u32[]{:S(2)}) %collective-permute-start.5) | collective-permute-done | bytes 311328 | tf_op jit(solution)/shard_map/ppermute | solution.py:362
  180.4 11.7 %shard_map.18 = (bf16[2,3072,256]{2,1,0:T(8,128)(2,1)}, bf16[2,3072,256]{2,1,0:T(8,128)(2,1)}, f32[256,256]{1,0:T(8,128)}) custom-call(bf16[2,24,128,256]{3,2,1,0:T(8,128)(2,1)} %collective-permute-done.4.refs_0_, bf16[2,2,152,256]{3,2,1,0:T(8,128)(2,1)} %collective-permute-done.5.refs_1_, bf16[2,3072,256]{2,1,0:T(8,128)(2,1)} %get-tuple-element.18.refs_2_.refs_0_, ...), custom_call_target="tpu_custom_call" | custom-call | tf_op jit(solution)/shard_map/pallas_call | solution.py:292
  192.1 2.6 shard_map.22
  194.7 11.1 %all_to_all.71 = f32[8,16,128]{2,1,0:T(8,128)S(1)} all-to-all(f32[8,16,128]{2,1,0:T(8,128)} %bitcast.23), channel_id=1, replica_groups=mesh['gx'=8,'gy'=8,'cyc'=4] {'gx'}, dimensions={0} | all-to-all | bytes 131072 | tf_op jit(solution)/shard_map/all_to_all | solution.py:367
  205.8 15.1 %all_to_all.72 = f32[8,16,128]{2,1,0:T(8,128)S(1)} all-to-all(f32[8,16,128]{2,1,0:T(8,128)S(1)} %broadcast_in_dim.14), channel_id=1, replica_groups=mesh['gx'=8,'gy'=8,'cyc'=4] {'gy'}, dimensions={0} | all-to-all | bytes 131072 | tf_op jit(solution)/shard_map/all_to_all | solution.py:374
  220.9 10.1 %all_to_all.73 = f32[8,16,128]{2,1,0:T(8,128)} all-to-all(f32[8,16,128]{2,1,0:T(8,128)S(1)} %broadcast_in_dim.15), channel_id=1, replica_groups=mesh['gx'=8,'gy'=8,'cyc'=4] {'gx'}, dimensions={0} | all-to-all | bytes 131072 | tf_op jit(solution)/shard_map/all_to_all | solution.py:374
  231.0 18.5 %shard_map.23.own_ref = f32[640,128]{1,0:T(8,128)} custom-call(f32[384,128]{1,0:T(8,128)} %shard_map.21.own_ref, f32[128,128]{1,0:T(8,128)} %bitcast.21, f32[384,128]{1,0:T(8,128)} %collective-permute-done.10.far_ref), custom_call_target="tpu_custom_call" | custom-call | tf_op jit(solution)/shard_map/pallas_call | solution.py:157
  249.5 0.6 collective-permute-start.11
  250.1 1.7 collective-permute-start.9
  251.8 0.7 collective-permute-start.8
  252.5 21.7 %collective-permute-done.9.refs_1_ = bf16[2,2,152,256]{3,2,1,0:T(8,128)(2,1)S(1)} collective-permute-done((bf16[2,2,152,256]{3,2,1,0:T(8,128)(2,1)S(1)}, bf16[2,2,152,256]{3,2,1,0:T(8,128)(2,1)S(1)}, u32[]{:S(2)}, u32[]{:S(2)}) %collective-permute-start.9) | collective-permute-done | bytes 311328 | tf_op jit(solution)/shard_map/ppermute | solution.py:362
  274.2 0.7 copy-done.4
  275.0 14.3 %shard_map.20 = (bf16[2,3072,256]{2,1,0:T(8,128)(2,1)}, bf16[2,3072,256]{2,1,0:T(8,128)(2,1)}, f32[256,512]{1,0:T(8,128)}) custom-call(bf16[2,24,128,256]{3,2,1,0:T(8,128)(2,1)} %collective-permute-done.6.refs_0_, bf16[2,2,152,256]{3,2,1,0:T(8,128)(2,1)} %copy-done.4, bf16[2,3072,256]{2,1,0:T(8,128)(2,1)} %get-tuple-element.18.refs_2_.refs_0_, ...), custom_call_target="tpu_custom_call" | custom-call | tf_op jit(solution)/shard_map/pallas_call | solution.py:292
  289.3 0.7 copy-done.3
  290.0 14.3 %shard_map.19 = (bf16[2,3072,256]{2,1,0:T(8,128)(2,1)}, bf16[2,3072,256]{2,1,0:T(8,128)(2,1)}, f32[256,512]{1,0:T(8,128)}) custom-call(bf16[2,24,128,256]{3,2,1,0:T(8,128)(2,1)} %collective-permute-done.7.refs_0_, bf16[2,2,152,256]{3,2,1,0:T(8,128)(2,1)} %copy-done.3, bf16[2,3072,256]{2,1,0:T(8,128)(2,1)} %get-tuple-element.18.refs_2_.refs_0_, ...), custom_call_target="tpu_custom_call" | custom-call | tf_op jit(solution)/shard_map/pallas_call | solution.py:292
  304.4 0.7 copy-done.1
  305.1 3.4 shard_map.24
  308.5 8.6 %all_to_all.74 = f32[8,16,128]{2,1,0:T(8,128)S(1)} all-to-all(f32[8,16,128]{2,1,0:T(8,128)} %bitcast.20), channel_id=1, replica_groups=mesh['gx'=8,'gy'=8,'cyc'=4] {'gx'}, dimensions={0} | all-to-all | bytes 131072 | tf_op jit(solution)/shard_map/all_to_all | solution.py:367
  317.1 0.6 broadcast_in_dim.16
  317.7 3.4 all-to-all-start.7
  321.1 7.1 %all-to-all-done.7 = f32[8,16,128]{2,1,0:T(8,128)S(1)} async-done(((f32[8,16,128]{2,1,0:T(8,128)}), f32[8,16,128]{2,1,0:T(8,128)S(1)}, u32[]{:S(2)}, u32[]{:S(2)}) %all-to-all-start.7) | async-done | bytes 65568 | tf_op jit(solution)/shard_map/all_to_all | solution.py:374
  328.3 0.6 broadcast_in_dim.17
  328.9 5.2 %all-to-all-start.8 = ((f32[8,16,128]{2,1,0:T(8,128)}), f32[8,16,128]{2,1,0:T(8,128)S(1)}, u32[]{:S(2)}, u32[]{:S(2)}) async-start(f32[8,16,128]{2,1,0:T(8,128)} %broadcast_in_dim.17), calls=%async_computation.8 | async-start | bytes 131072 | tf_op jit(solution)/shard_map/all_to_all | solution.py:374
  334.1 0.7 fusion.pick_ref
  334.8 4.2 %all-to-all-done.8 = f32[8,16,128]{2,1,0:T(8,128)S(1)} async-done(((f32[8,16,128]{2,1,0:T(8,128)}), f32[8,16,128]{2,1,0:T(8,128)S(1)}, u32[]{:S(2)}, u32[]{:S(2)}) %all-to-all-start.8) | async-done | bytes 65568 | tf_op jit(solution)/shard_map/all_to_all | solution.py:374
  339.0 0.6 copy-done.5
  339.6 18.7 %shard_map.25.refs_8_ = bf16[64,1024]{1,0:T(8,128)(2,1)} custom-call(f32[640,128]{1,0:T(8,128)} %shard_map.23.own_ref, f32[128,128]{1,0:T(8,128)} %bitcast.22, f32[640,128]{1,0:T(8,128)} %copy-done.1, f32[32,128]{1,0:T(8,128)} %fusion.pick_ref), custom_call_target="tpu_custom_call" | custom-call | tf_op jit(solution)/shard_map/pallas_call | solution.py:179
  358.3 13.6 %shard_map.26 = f32[2,24,32,128]{3,2,1,0:T(8,128)} custom-call(bf16[2,3072,256]{2,1,0:T(8,128)(2,1)} %get-tuple-element.18.refs_2_.refs_0_, bf16[2,3072,256]{2,1,0:T(8,128)(2,1)} %get-tuple-element.19.refs_3_.refs_1_, bf16[2,3072,256]{2,1,0:T(8,128)(2,1)} %get-tuple-element.20.refs_4_.refs_2_, bf16[2,3072,256]{2,1,0:T(8,128)(2,1)} %get-tuple-element.21.refs_5_.refs_3_, ...), custom_call_target="tpu_custom_call" | custom-call | tf_op jit(solution)/shard_map/pallas_call | solution.py:329
  (31 shorter events, 0.2 us)
Async XLA Ops:
  0.0 36.6 %copy-start = (bf16[2,24,128,256]{3,2,1,0:T(8,128)(2,1)S(1)}, bf16[2,24,128,256]{3,2,1,0:T(8,128)(2,1)}, u32[]{:S(2)}) copy-start(bf16[2,24,128,256]{3,2,1,0:T(8,128)(2,1)} %refs_0_.1) | copy-start | bytes 9437188
  0.0 72.8 %collective-permute-start.6 = (bf16[2,24,128,256]{3,2,1,0:T(8,128)(2,1)}, bf16[2,24,128,256]{3,2,1,0:T(8,128)(2,1)}, u32[]{:S(2)}, u32[]{:S(2)}) collective-permute-start(bf16[2,24,128,256]{3,2,1,0:T(8,128)(2,1)} %refs_0_.1), channel_id=1, source_target_pairs={{0,3},{1,2},{2,1},{3,0},{4,7},{5,6},{6,5},{7,4},{8,11},{9,10},{10,... | collective-permute-start | bytes 9437192 | tf_op jit(solution)/shard_map/ppermute | solution.py:362
  4.6 11.9 %collective-permute-start = (bf16[2,1,128,256]{3,2,0,1:T(8,128)(2,1)S(1)}, bf16[2,1,128,256]{3,2,0,1:T(8,128)(2,1)S(1)}, u32[]{:S(2)}, u32[]{:S(2)}) collective-permute-start(bf16[2,1,128,256]{3,2,0,1:T(8,128)(2,1)S(1)} %get-tuple-element.31), channel_id=1, source_target_pairs={{0,32},{32,64},{64,96},{96,128},{128,160},{160,192},{192,224},{1,3... | collective-permute-start | bytes 393224 | tf_op jit(solution)/shard_map/ppermute | solution.py:344
  9.6 6.8 %collective-permute-start.1 = (bf16[2,24,1,256]{3,1,0,2:T(8,128)(2,1)S(1)}, bf16[2,24,1,256]{3,1,0,2:T(8,128)(2,1)S(1)}, u32[]{:S(2)}, u32[]{:S(2)}) collective-permute-start(bf16[2,24,1,256]{3,1,0,2:T(8,128)(2,1)S(1)} %copy.11), channel_id=1, source_target_pairs={{0,4},{4,8},{8,12},{12,16},{16,20},{20,24},{24,28},{1,5},{5,9},{9,... | collective-permute-start | bytes 73736 | tf_op jit(solution)/shard_map/ppermute | solution.py:344
  13.2 7.1 %collective-permute-start.2 = (bf16[2,1,128,256]{3,2,0,1:T(8,128)(2,1)S(1)}, bf16[2,1,128,256]{3,2,0,1:T(8,128)(2,1)S(1)}, u32[]{:S(2)}, u32[]{:S(2)}) collective-permute-start(bf16[2,1,128,256]{3,2,0,1:T(8,128)(2,1)S(1)} %get-tuple-element.32), channel_id=1, source_target_pairs={{32,0},{64,32},{96,64},{128,96},{160,128},{192,160},{224,192},{33,... | collective-permute-start | bytes 393224 | tf_op jit(solution)/shard_map/ppermute | solution.py:347
  15.1 5.2 %collective-permute-start.3 = (bf16[2,24,1,256]{3,1,0,2:T(8,128)(2,1)S(1)}, bf16[2,24,1,256]{3,1,0,2:T(8,128)(2,1)S(1)}, u32[]{:S(2)}, u32[]{:S(2)}) collective-permute-start(bf16[2,24,1,256]{3,1,0,2:T(8,128)(2,1)S(1)} %copy.13), channel_id=1, source_target_pairs={{4,0},{8,4},{12,8},{16,12},{20,16},{24,20},{28,24},{5,1},{9,5},{13... | collective-permute-start | bytes 73736 | tf_op jit(solution)/shard_map/ppermute | solution.py:347
  21.1 51.8 %copy-start.2 = (bf16[2,2,152,256]{3,2,1,0:T(8,128)(2,1)S(1)}, bf16[2,2,152,256]{3,2,1,0:T(8,128)(2,1)}, u32[]{:S(2)}) copy-start(bf16[2,2,152,256]{3,2,1,0:T(8,128)(2,1)} %pad_maximum_fusion.refs_1_) | copy-start | bytes 933892
  31.1 11.5 %all-to-all-start = ((f32[8,48,128]{2,1,0:T(8,128)}), f32[8,48,128]{2,1,0:T(8,128)}, u32[]{:S(2)}, u32[]{:S(2)}) async-start(f32[8,48,128]{2,1,0:T(8,128)} %bitcast.24), calls=%async_computation | async-start | bytes 393216 | tf_op jit(solution)/shard_map/all_to_all | solution.py:367
  36.6 143.8 %collective-permute-start.4 = (bf16[2,24,128,256]{3,2,1,0:T(8,128)(2,1)S(1)}, bf16[2,24,128,256]{3,2,1,0:T(8,128)(2,1)}, u32[]{:S(2)}, u32[]{:S(2)}) collective-permute-start(bf16[2,24,128,256]{3,2,1,0:T(8,128)(2,1)S(1)} %copy-done), channel_id=1, source_target_pairs={{0,1},{1,0},{2,3},{3,2},{4,5},{5,4},{6,7},{7,6},{8,9},{9,8},{10,11... | collective-permute-start | bytes 9437192 | tf_op jit(solution)/shard_map/ppermute | solution.py:362
  72.8 216.5 %collective-permute-start.7 = (bf16[2,24,128,256]{3,2,1,0:T(8,128)(2,1)}, bf16[2,24,128,256]{3,2,1,0:T(8,128)(2,1)}, u32[]{:S(2)}, u32[]{:S(2)}) collective-permute-start(bf16[2,24,128,256]{3,2,1,0:T(8,128)(2,1)} %collective-permute-done.6.refs_0_), channel_id=1, source_target_pairs={{0,1},{1,0},{2,3},{3,2},{4,5},{5,4},{6,7},{7,6},{8,9},{9,8},{10,11... | collective-permute-start | bytes 9437192 | tf_op jit(solution)/shard_map/ppermute | solution.py:362
  72.8 107.5 %collective-permute-start.5 = (bf16[2,2,152,256]{3,2,1,0:T(8,128)(2,1)S(1)}, bf16[2,2,152,256]{3,2,1,0:T(8,128)(2,1)}, u32[]{:S(2)}, u32[]{:S(2)}) collective-permute-start(bf16[2,2,152,256]{3,2,1,0:T(8,128)(2,1)S(1)} %copy-done.2), channel_id=1, source_target_pairs={{0,1},{1,0},{2,3},{3,2},{4,5},{5,4},{6,7},{7,6},{8,9},{9,8},{10,11... | collective-permute-start | bytes 933896 | tf_op jit(solution)/shard_map/ppermute | solution.py:362
  92.4 99.7 %collective-permute-start.10 = (f32[384,128]{1,0:T(8,128)}, f32[384,128]{1,0:T(8,128)}, u32[]{:S(2)}, u32[]{:S(2)}) collective-permute-start(f32[384,128]{1,0:T(8,128)} %shard_map.21.own_ref), channel_id=1, source_target_pairs={{0,1},{1,0},{2,3},{3,2},{4,5},{5,4},{6,7},{7,6},{8,9},{9,8},{10,11... | collective-permute-start | bytes 589832 | tf_op jit(solution)/shard_map/ppermute | solution.py:362
  249.5 54.8 %collective-permute-start.11 = (f32[640,128]{1,0:T(8,128)}, f32[640,128]{1,0:T(8,128)S(1)}, u32[]{:S(2)}, u32[]{:S(2)}) collective-permute-start(f32[640,128]{1,0:T(8,128)} %shard_map.23.own_ref), channel_id=1, source_target_pairs={{0,2},{1,3},{2,0},{3,1},{4,6},{5,7},{6,4},{7,5},{8,10},{9,11},{10,... | collective-permute-start | bytes 983048 | tf_op jit(solution)/shard_map/ppermute | solution.py:362
  250.1 24.1 %collective-permute-start.9 = (bf16[2,2,152,256]{3,2,1,0:T(8,128)(2,1)S(1)}, bf16[2,2,152,256]{3,2,1,0:T(8,128)(2,1)S(1)}, u32[]{:S(2)}, u32[]{:S(2)}) collective-permute-start(bf16[2,2,152,256]{3,2,1,0:T(8,128)(2,1)S(1)} %copy-done.2), channel_id=1, source_target_pairs={{0,3},{1,2},{2,1},{3,0},{4,7},{5,6},{6,5},{7,4},{8,11},{9,10},{10,... | collective-permute-start | bytes 933896 | tf_op jit(solution)/shard_map/ppermute | solution.py:362
  251.8 37.5 %collective-permute-start.8 = (bf16[2,2,152,256]{3,2,1,0:T(8,128)(2,1)S(1)}, bf16[2,2,152,256]{3,2,1,0:T(8,128)(2,1)S(1)}, u32[]{:S(2)}, u32[]{:S(2)}) collective-permute-start(bf16[2,2,152,256]{3,2,1,0:T(8,128)(2,1)S(1)} %copy-done.2), channel_id=1, source_target_pairs={{0,2},{1,3},{2,0},{3,1},{4,6},{5,7},{6,4},{7,5},{8,10},{9,11},{10,... | collective-permute-start | bytes 933896 | tf_op jit(solution)/shard_map/ppermute | solution.py:362
  274.2 0.7 copy-start.4
  289.3 0.7 copy-start.3
  304.4 0.7 copy-start.1
  317.7 10.5 %all-to-all-start.7 = ((f32[8,16,128]{2,1,0:T(8,128)}), f32[8,16,128]{2,1,0:T(8,128)S(1)}, u32[]{:S(2)}, u32[]{:S(2)}) async-start(f32[8,16,128]{2,1,0:T(8,128)} %broadcast_in_dim.16), calls=%async_computation.7 | async-start | bytes 131072 | tf_op jit(solution)/shard_map/all_to_all | solution.py:374
  328.9 10.1 %all-to-all-start.8 = ((f32[8,16,128]{2,1,0:T(8,128)}), f32[8,16,128]{2,1,0:T(8,128)S(1)}, u32[]{:S(2)}, u32[]{:S(2)}) async-start(f32[8,16,128]{2,1,0:T(8,128)} %broadcast_in_dim.17), calls=%async_computation.8 | async-start | bytes 131072 | tf_op jit(solution)/shard_map/all_to_all | solution.py:374
  339.0 0.6 copy-start.5
where the time goes:
time: 373 us; the launch traced here: 372 us
  waiting for transfers between devices  131 us (35%)
  Pallas kernels  125 us (34%)
  blocking collectives  73.1 us (20%)
  starting transfers between devices  32.8 us (9%)
  local copies, waits for them, and re-layouts  6.23 us (2%)
    ppermute x8, waiting for transfers between devices, swapped(): return lax.ppermute(value, 'cyc', pairs)  110 us
    all_to_all x4, blocking collectives, gathered(): lax.all_to_all(copies.reshape(-1, value.shape[1]), axis, 0, 0, tiled=True)  53.5 us
    pallas_call x4, Pallas kernels, features(): pl.pallas_call(lambda *refs: feature_kernel(count, *refs), grid=(height /...  50.5 us
    all_to_all x2, blocking collectives, scatter_sum(): parts = lax.all_to_all(value, axis, 0, 0, tiled=True)  19.6 us
    pallas_call x1, Pallas kernels, last_level(): pl.pallas_call(last_kernel, out_shape=jax.ShapeDtypeStruct((2 * pick.shap...  18.7 us
    pallas_call x1, Pallas kernels, next_level(): pl.pallas_call(level_kernel, out_shape=jax.ShapeDtypeStruct((2 * w + RANK...  18.5 us
    pallas_call x1, Pallas kernels, first_level(): pl.pallas_call(first_kernel, out_shape=jax.ShapeDtypeStruct((3 * RANK, RA...  18.1 us
    pallas_call x1, Pallas kernels, finish(): pl.pallas_call(finish_kernel, grid=(2, height // rows), in_specs=[part] *...  13.6 us
  transfers between devices with their start and end apart: 15, of which 6 were waited for; matrix products, arithmetic and copies ran while one was open for 1% of the time, Pallas kernels for 24%

commit v1 on v0

--- a/solution.py
+++ b/solution.py
@@ -349,7 +349,6 @@
 
 
 def halo_of(block):
-    _, height, wide, snaps = block.shape
     x_low, x_high = edges(block, "gx", 1)
     y_low, y_high = edges(block, "gy", 2)
     low = jnp.concatenate([x_low[:, 0], y_low[:, :, 0]], axis=1)
@@ -381,23 +380,25 @@
     return gathered(part, "gx").reshape(value.shape)
 
 
-def on_device(displacement):
+def whole(displacement):
     _, height, wide, _ = displacement.shape
     groups = lax.axis_size("cyc")
     halo = halo_of(displacement)
     near = swapped(displacement, 1)
     side = swapped(displacement, 3)
+    near_halo, far_halo, side_halo = (swapped(halo, mask) for mask in (1, 2, 3))
     own, gram = features(displacement, halo, [])
     total = all_sum(gram)
-    relayed, _ = lax.optimization_barrier((side, total))
-    far = swapped(relayed, 1)
     level0 = first_level(total)
-    pair, cross1 = features(near, swapped(halo, 1), [own])
     other0 = swapped(level0, 1)
-    level1 = next_level(level0, all_sum(project(level0, other0, [cross1])), other0)
-    fourth, cross3 = features(side, swapped(halo, 3), [own, pair])
-    third, cross2 = features(far, swapped(halo, 2), [own, pair])
+    relayed, _ = lax.optimization_barrier((near, total))
+    far = swapped(relayed, 3)
+    pair, cross1 = features(near, near_halo, [own])
+    total = all_sum(project(level0, other0, [cross1]))
+    level1 = next_level(level0, total, other0)
     other1 = swapped(level1, 2)
+    fourth, cross3 = features(side, side_halo, [own, pair])
+    third, cross2 = features(far, far_halo, [own, pair])
     share = RANK // groups
     column = lax.axis_index("cyc") * share + jnp.arange(share)
     pick = (column[:, None] == jnp.arange(RANK)[None, :]).astype(F32)
@@ -409,7 +410,7 @@
 
 def solution(mesh):
     return jax.shard_map(
-        on_device,
+        whole,
         mesh=mesh,
         in_specs=(P(None, "gx", "gy", "cyc"),),
         out_specs=P(None, "gx", "gy", "cyc"),

time: 373 us -> 327 us (0.88)
  waiting for transfers between devices: 131 us -> 79.8 us
    ppermute x8, waiting for transfers between devices: 110 us -> 60.6 us  [swapped(): return lax.ppermute(value, 'cyc', pairs)]
    all_to_all x4 -> x3, blocking collectives: 53.5 us -> 41.2 us  [gathered(): lax.all_to_all(copies.reshape(-1, value.shape[1]), axis, 0, 0, tiled=True)]
    all_to_all x2 -> x3, blocking collectives: 19.6 us -> 31.7 us  [scatter_sum(): parts = lax.all_to_all(value, axis, 0, 0, tiled=True)]
    all_to_all x2 -> x3, starting transfers between devices: 8.53 us -> 15.2 us  [gathered(): lax.all_to_all(copies.reshape(-1, value.shape[1]), axis, 0, 0, tiled=True)]
    all_to_all x1 -> x0, waiting for transfers between devices: 5.95 us -> none  [scatter_sum(): parts = lax.all_to_all(value, axis, 0, 0, tiled=True)]
    all_to_all x1 -> x0, starting transfers between devices: 5.5 us -> none  [scatter_sum(): parts = lax.all_to_all(value, axis, 0, 0, tiled=True)]
    all_to_all x2 -> x3, waiting for transfers between devices: 11.3 us -> 15.4 us  [gathered(): lax.all_to_all(copies.reshape(-1, value.shape[1]), axis, 0, 0, tiled=True)]
  transfers between devices with their start and end apart: 15 -> 15, of which waited for: 6 -> 5; matrix products, arithmetic and copies ran while one was open for 1% -> 2% of each run, Pallas kernels for 24% -> 28%
where the time goes in v1:
time: 327 us; the launch traced here: 325 us
  Pallas kernels  126 us (39%)
  waiting for transfers between devices  79.8 us (24%)
  blocking collectives  72.9 us (22%)
  starting transfers between devices  36.3 us (11%)
  local copies, waits for them, and re-layouts  6.94 us (2%)
  other arithmetic  3.38 us (1%)
    ppermute x8, waiting for transfers between devices, swapped(): return lax.ppermute(value, 'cyc', pairs)  60.6 us
    pallas_call x4, Pallas kernels, features(): pl.pallas_call(lambda *refs: feature_kernel(count, *refs), grid=(height /...  50.7 us
    all_to_all x3, blocking collectives, gathered(): lax.all_to_all(copies.reshape(-1, value.shape[1]), axis, 0, 0, tiled=True)  41.2 us
    all_to_all x3, blocking collectives, scatter_sum(): parts = lax.all_to_all(value, axis, 0, 0, tiled=True)  31.7 us
    pallas_call x1, Pallas kernels, last_level(): pl.pallas_call(last_kernel, out_shape=jax.ShapeDtypeStruct((2 * pick.shap...  18.7 us
    pallas_call x1, Pallas kernels, next_level(): pl.pallas_call(level_kernel, out_shape=jax.ShapeDtypeStruct((2 * w + RANK...  18.5 us
    pallas_call x1, Pallas kernels, first_level(): pl.pallas_call(first_kernel, out_shape=jax.ShapeDtypeStruct((3 * RANK, RA...  18.1 us
    all_to_all x3, waiting for transfers between devices, gathered(): lax.all_to_all(copies.reshape(-1, value.shape[1]), axis, 0, 0, tiled=True)  15.4 us
  transfers between devices with their start and end apart: 15, of which 5 were waited for; matrix products, arithmetic and copies ran while one was open for 2% of the time, Pallas kernels for 28%

profile of v1, /device:TPU:1, one launch (start us, length us, event | category | flops | bytes accessed | tf_op | source)
XLA Modules:
  0.0 325.1 jit_solution(16104742231412260474)
XLA Ops:
  0.0 2.1 collective-permute-start.4
  2.1 1.0 slice_bitcast_fusion.1
  3.1 4.0 %collective-permute-start = (bf16[2,1,128,256]{3,2,0,1:T(8,128)(2,1)S(1)}, bf16[2,1,128,256]{3,2,0,1:T(8,128)(2,1)S(1)}, u32[]{:S(2)}, u32[]{:S(2)}) collective-permute-start(bf16[2,1,128,256]{3,2,0,1:T(8,128)(2,1)S(1)} %get-tuple-element.31), channel_id=1, source_target_pairs={{0,32},{32,64},{64,96},{96,128},{128,160},{160,192},{192,224},{1,3... | collective-permute-start | bytes 393224 | tf_op jit(solution)/shard_map/ppermute | solution.py:344
  7.1 1.1 fusion.1
  8.2 3.5 %collective-permute-start.1 = (bf16[2,24,1,256]{3,1,0,2:T(8,128)(2,1)S(1)}, bf16[2,24,1,256]{3,1,0,2:T(8,128)(2,1)S(1)}, u32[]{:S(2)}, u32[]{:S(2)}) collective-permute-start(bf16[2,24,1,256]{3,1,0,2:T(8,128)(2,1)S(1)} %copy.11), channel_id=1, source_target_pairs={{0,4},{4,8},{8,12},{12,16},{16,20},{20,24},{24,28},{1,5},{5,9},{9,... | collective-permute-start | bytes 73736 | tf_op jit(solution)/shard_map/ppermute | solution.py:344
  11.8 1.9 collective-permute-start.2
  13.7 1.3 collective-permute-start.3
  15.0 3.8 %collective-permute-done.3 = bf16[2,24,1,256]{3,1,0,2:T(8,128)(2,1)S(1)} collective-permute-done((bf16[2,24,1,256]{3,1,0,2:T(8,128)(2,1)S(1)}, bf16[2,24,1,256]{3,1,0,2:T(8,128)(2,1)S(1)}, u32[]{:S(2)}, u32[]{:S(2)}) %collective-permute-start.3) | collective-permute-done | bytes 24608 | tf_op jit(solution)/shard_map/ppermute | solution.py:347
  18.9 0.8 pad_maximum_fusion.refs_1_
  19.6 10.3 %shard_map.17 = (bf16[2,3072,256]{2,1,0:T(8,128)(2,1)}, bf16[2,3072,256]{2,1,0:T(8,128)(2,1)}, f32[384,128]{1,0:T(8,128)}) custom-call(bf16[2,24,128,256]{3,2,1,0:T(8,128)(2,1)} %refs_0_.1, bf16[2,2,152,256]{3,2,1,0:T(8,128)(2,1)} %pad_maximum_fusion.refs_1_), custom_call_target="tpu_custom_call" | custom-call | tf_op jit(solution)/shard_map/pallas_call | solution.py:292
  29.9 11.5 %all_to_all.69 = f32[8,48,128]{2,1,0:T(8,128)} all-to-all(f32[8,48,128]{2,1,0:T(8,128)} %bitcast.23), channel_id=1, replica_groups=mesh['gx'=8,'gy'=8,'cyc'=4] {'gx'}, dimensions={0} | all-to-all | bytes 393216 | tf_op jit(solution)/shard_map/all_to_all | solution.py:366
  41.4 0.9 reduce_sum.54
  42.4 16.6 %all_to_all.70 = f32[8,48,128]{2,1,0:T(8,128)} all-to-all(f32[8,48,128]{2,1,0:T(8,128)S(1)} %broadcast_in_dim.12), channel_id=1, replica_groups=mesh['gx'=8,'gy'=8,'cyc'=4] {'gy'}, dimensions={0} | all-to-all | bytes 393216 | tf_op jit(solution)/shard_map/all_to_all | solution.py:373
  58.9 0.9 reduce_sum.55
  59.9 0.7 broadcast_in_dim.13
  60.6 6.7 %all-to-all-start.2 = ((f32[8,48,128]{2,1,0:T(8,128)}), f32[8,48,128]{2,1,0:T(8,128)}, u32[]{:S(2)}, u32[]{:S(2)}) async-start(f32[8,48,128]{2,1,0:T(8,128)} %broadcast_in_dim.13), calls=%async_computation.2 | async-start | bytes 393216 | tf_op jit(solution)/shard_map/all_to_all | solution.py:373
  67.3 1.9 collective-permute-start.8
  69.2 4.1 %all-to-all-done.2 = f32[8,48,128]{2,1,0:T(8,128)} async-done(((f32[8,48,128]{2,1,0:T(8,128)}), f32[8,48,128]{2,1,0:T(8,128)}, u32[]{:S(2)}, u32[]{:S(2)}) %all-to-all-start.2) | async-done | bytes 196640 | tf_op jit(solution)/shard_map/all_to_all | solution.py:373
  73.3 1.9 collective-permute-start.6
  75.2 0.4 collective-permute-start.5
  75.6 18.1 %shard_map.21.own_ref = f32[384,128]{1,0:T(8,128)} custom-call(f32[384,128]{1,0:T(8,128)} %bitcast.7.g_ref), custom_call_target="tpu_custom_call" | custom-call | tf_op jit(solution)/shard_map/pallas_call | solution.py:133
  93.7 1.1 collective-permute-start.10
  94.8 11.7 %shard_map.18 = (bf16[2,3072,256]{2,1,0:T(8,128)(2,1)}, bf16[2,3072,256]{2,1,0:T(8,128)(2,1)}, f32[256,256]{1,0:T(8,128)}) custom-call(bf16[2,24,128,256]{3,2,1,0:T(8,128)(2,1)} %collective-permute-done.4.refs_0_, bf16[2,2,152,256]{3,2,1,0:T(8,128)(2,1)} %collective-permute-done.5.refs_1_, bf16[2,3072,256]{2,1,0:T(8,128)(2,1)} %get-tuple-element.18.refs_2_.refs_0_, ...), custom_call_target="tpu_custom_call" | custom-call | tf_op jit(solution)/shard_map/pallas_call | solution.py:292
  106.5 2.6 shard_map.22
  109.1 9.9 %all_to_all.71 = f32[8,16,128]{2,1,0:T(8,128)S(1)} all-to-all(f32[8,16,128]{2,1,0:T(8,128)} %bitcast.22), channel_id=1, replica_groups=mesh['gx'=8,'gy'=8,'cyc'=4] {'gx'}, dimensions={0} | all-to-all | bytes 131072 | tf_op jit(solution)/shard_map/all_to_all | solution.py:366
  119.0 14.5 %all_to_all.72 = f32[8,16,128]{2,1,0:T(8,128)S(1)} all-to-all(f32[8,16,128]{2,1,0:T(8,128)S(1)} %broadcast_in_dim.14), channel_id=1, replica_groups=mesh['gx'=8,'gy'=8,'cyc'=4] {'gy'}, dimensions={0} | all-to-all | bytes 131072 | tf_op jit(solution)/shard_map/all_to_all | solution.py:373
  133.6 10.1 %all_to_all.73 = f32[8,16,128]{2,1,0:T(8,128)} all-to-all(f32[8,16,128]{2,1,0:T(8,128)S(1)} %broadcast_in_dim.15), channel_id=1, replica_groups=mesh['gx'=8,'gy'=8,'cyc'=4] {'gx'}, dimensions={0} | all-to-all | bytes 131072 | tf_op jit(solution)/shard_map/all_to_all | solution.py:373
  143.7 18.5 %shard_map.23.own_ref = f32[640,128]{1,0:T(8,128)} custom-call(f32[384,128]{1,0:T(8,128)} %shard_map.21.own_ref, f32[128,128]{1,0:T(8,128)} %bitcast.20, f32[384,128]{1,0:T(8,128)} %collective-permute-done.10.far_ref), custom_call_target="tpu_custom_call" | custom-call | tf_op jit(solution)/shard_map/pallas_call | solution.py:157
  162.5 1.9 collective-permute-start.9
  164.4 0.7 collective-permute-start.7
  165.2 60.5 %collective-permute-done.9.refs_1_ = bf16[2,2,152,256]{3,2,1,0:T(8,128)(2,1)S(1)} collective-permute-done((bf16[2,2,152,256]{3,2,1,0:T(8,128)(2,1)}, bf16[2,2,152,256]{3,2,1,0:T(8,128)(2,1)S(1)}, u32[]{:S(2)}, u32[]{:S(2)}) %collective-permute-start.9) | collective-permute-done | bytes 311328 | tf_op jit(solution)/shard_map/ppermute | solution.py:361
  225.7 0.7 copy-done.4
  226.5 14.4 %shard_map.20 = (bf16[2,3072,256]{2,1,0:T(8,128)(2,1)}, bf16[2,3072,256]{2,1,0:T(8,128)(2,1)}, f32[256,512]{1,0:T(8,128)}) custom-call(bf16[2,24,128,256]{3,2,1,0:T(8,128)(2,1)} %collective-permute-done.8.refs_0_, bf16[2,2,152,256]{3,2,1,0:T(8,128)(2,1)} %copy-done.4, bf16[2,3072,256]{2,1,0:T(8,128)(2,1)} %get-tuple-element.18.refs_2_.refs_0_, ...), custom_call_target="tpu_custom_call" | custom-call | tf_op jit(solution)/shard_map/pallas_call | solution.py:292
  240.8 0.7 copy-done.3
  241.6 14.3 %shard_map.19 = (bf16[2,3072,256]{2,1,0:T(8,128)(2,1)}, bf16[2,3072,256]{2,1,0:T(8,128)(2,1)}, f32[256,512]{1,0:T(8,128)}) custom-call(bf16[2,24,128,256]{3,2,1,0:T(8,128)(2,1)} %collective-permute-done.6.refs_0_, bf16[2,2,152,256]{3,2,1,0:T(8,128)(2,1)} %copy-done.3, bf16[2,3072,256]{2,1,0:T(8,128)(2,1)} %get-tuple-element.18.refs_2_.refs_0_, ...), custom_call_target="tpu_custom_call" | custom-call | tf_op jit(solution)/shard_map/pallas_call | solution.py:292
  255.9 0.7 copy-done.1
  256.6 3.4 %shard_map.24 = f32[128,128]{1,0:T(8,128)} custom-call(f32[640,128]{1,0:T(8,128)} %shard_map.23.own_ref, f32[640,128]{1,0:T(8,128)} %copy-done.1, f32[256,512]{1,0:T(8,128)} %get-tuple-element.29.refs_0_, f32[256,512]{1,0:T(8,128)} %get-tuple-element.30.refs_1_), custom_call_target="tpu_custom_call" | custom-call | tf_op jit(solution)/shard_map/pallas_call | solution.py:199
  260.0 10.4 %all_to_all.74 = f32[8,16,128]{2,1,0:T(8,128)S(1)} all-to-all(f32[8,16,128]{2,1,0:T(8,128)} %bitcast.19), channel_id=1, replica_groups=mesh['gx'=8,'gy'=8,'cyc'=4] {'gx'}, dimensions={0} | all-to-all | bytes 131072 | tf_op jit(solution)/shard_map/all_to_all | solution.py:366
  270.4 0.6 broadcast_in_dim.16
  271.1 3.4 %all-to-all-start.7 = ((f32[8,16,128]{2,1,0:T(8,128)}), f32[8,16,128]{2,1,0:T(8,128)S(1)}, u32[]{:S(2)}, u32[]{:S(2)}) async-start(f32[8,16,128]{2,1,0:T(8,128)} %broadcast_in_dim.16), calls=%async_computation.7 | async-start | bytes 131072 | tf_op jit(solution)/shard_map/all_to_all | solution.py:373
  274.4 7.1 %all-to-all-done.7 = f32[8,16,128]{2,1,0:T(8,128)S(1)} async-done(((f32[8,16,128]{2,1,0:T(8,128)}), f32[8,16,128]{2,1,0:T(8,128)S(1)}, u32[]{:S(2)}, u32[]{:S(2)}) %all-to-all-start.7) | async-done | bytes 65568 | tf_op jit(solution)/shard_map/all_to_all | solution.py:373
  281.6 0.6 broadcast_in_dim.17
  282.2 5.2 %all-to-all-start.8 = ((f32[8,16,128]{2,1,0:T(8,128)}), f32[8,16,128]{2,1,0:T(8,128)S(1)}, u32[]{:S(2)}, u32[]{:S(2)}) async-start(f32[8,16,128]{2,1,0:T(8,128)} %broadcast_in_dim.17), calls=%async_computation.8 | async-start | bytes 131072 | tf_op jit(solution)/shard_map/all_to_all | solution.py:373
  287.4 0.7 fusion.pick_ref
  288.1 4.2 %all-to-all-done.8 = f32[8,16,128]{2,1,0:T(8,128)S(1)} async-done(((f32[8,16,128]{2,1,0:T(8,128)}), f32[8,16,128]{2,1,0:T(8,128)S(1)}, u32[]{:S(2)}, u32[]{:S(2)}) %all-to-all-start.8) | async-done | bytes 65568 | tf_op jit(solution)/shard_map/all_to_all | solution.py:373
  292.3 0.6 copy-done.5
  292.9 18.7 %shard_map.25.refs_8_ = bf16[64,1024]{1,0:T(8,128)(2,1)} custom-call(f32[640,128]{1,0:T(8,128)} %shard_map.23.own_ref, f32[128,128]{1,0:T(8,128)} %bitcast.21, f32[640,128]{1,0:T(8,128)} %copy-done.1, f32[32,128]{1,0:T(8,128)} %fusion.pick_ref), custom_call_target="tpu_custom_call" | custom-call | tf_op jit(solution)/shard_map/pallas_call | solution.py:179
  311.6 13.6 %shard_map.26 = f32[2,24,32,128]{3,2,1,0:T(8,128)} custom-call(bf16[2,3072,256]{2,1,0:T(8,128)(2,1)} %get-tuple-element.18.refs_2_.refs_0_, bf16[2,3072,256]{2,1,0:T(8,128)(2,1)} %get-tuple-element.19.refs_3_.refs_1_, bf16[2,3072,256]{2,1,0:T(8,128)(2,1)} %get-tuple-element.20.refs_4_.refs_2_, bf16[2,3072,256]{2,1,0:T(8,128)(2,1)} %get-tuple-element.21.refs_5_.refs_3_, ...), custom_call_target="tpu_custom_call" | custom-call | tf_op jit(solution)/shard_map/pallas_call | solution.py:329
  (31 shorter events, 0.5 us)
Async XLA Ops:
  0.0 73.3 %collective-permute-start.4 = (bf16[2,24,128,256]{3,2,1,0:T(8,128)(2,1)}, bf16[2,24,128,256]{3,2,1,0:T(8,128)(2,1)}, u32[]{:S(2)}, u32[]{:S(2)}) collective-permute-start(bf16[2,24,128,256]{3,2,1,0:T(8,128)(2,1)} %refs_0_.1), channel_id=1, source_target_pairs={{0,1},{1,0},{2,3},{3,2},{4,5},{5,4},{6,7},{7,6},{8,9},{9,8},{10,11... | collective-permute-start | bytes 9437192 | tf_op jit(solution)/shard_map/ppermute | solution.py:361
  3.1 11.9 %collective-permute-start = (bf16[2,1,128,256]{3,2,0,1:T(8,128)(2,1)S(1)}, bf16[2,1,128,256]{3,2,0,1:T(8,128)(2,1)S(1)}, u32[]{:S(2)}, u32[]{:S(2)}) collective-permute-start(bf16[2,1,128,256]{3,2,0,1:T(8,128)(2,1)S(1)} %get-tuple-element.31), channel_id=1, source_target_pairs={{0,32},{32,64},{64,96},{96,128},{128,160},{160,192},{192,224},{1,3... | collective-permute-start | bytes 393224 | tf_op jit(solution)/shard_map/ppermute | solution.py:344
  8.2 6.8 %collective-permute-start.1 = (bf16[2,24,1,256]{3,1,0,2:T(8,128)(2,1)S(1)}, bf16[2,24,1,256]{3,1,0,2:T(8,128)(2,1)S(1)}, u32[]{:S(2)}, u32[]{:S(2)}) collective-permute-start(bf16[2,24,1,256]{3,1,0,2:T(8,128)(2,1)S(1)} %copy.11), channel_id=1, source_target_pairs={{0,4},{4,8},{8,12},{12,16},{16,20},{20,24},{24,28},{1,5},{5,9},{9,... | collective-permute-start | bytes 73736 | tf_op jit(solution)/shard_map/ppermute | solution.py:344
  11.8 7.1 %collective-permute-start.2 = (bf16[2,1,128,256]{3,2,0,1:T(8,128)(2,1)S(1)}, bf16[2,1,128,256]{3,2,0,1:T(8,128)(2,1)S(1)}, u32[]{:S(2)}, u32[]{:S(2)}) collective-permute-start(bf16[2,1,128,256]{3,2,0,1:T(8,128)(2,1)S(1)} %get-tuple-element.32), channel_id=1, source_target_pairs={{32,0},{64,32},{96,64},{128,96},{160,128},{192,160},{224,192},{33,... | collective-permute-start | bytes 393224 | tf_op jit(solution)/shard_map/ppermute | solution.py:347
  13.7 5.2 %collective-permute-start.3 = (bf16[2,24,1,256]{3,1,0,2:T(8,128)(2,1)S(1)}, bf16[2,24,1,256]{3,1,0,2:T(8,128)(2,1)S(1)}, u32[]{:S(2)}, u32[]{:S(2)}) collective-permute-start(bf16[2,24,1,256]{3,1,0,2:T(8,128)(2,1)S(1)} %copy.13), channel_id=1, source_target_pairs={{4,0},{8,4},{12,8},{16,12},{20,16},{24,20},{28,24},{5,1},{9,5},{13... | collective-permute-start | bytes 73736 | tf_op jit(solution)/shard_map/ppermute | solution.py:347
  18.9 48.4 %copy-start = (bf16[2,24,128,256]{3,2,1,0:T(8,128)(2,1)S(1)}, bf16[2,24,128,256]{3,2,1,0:T(8,128)(2,1)}, u32[]{:S(2)}) copy-start(bf16[2,24,128,256]{3,2,1,0:T(8,128)(2,1)} %refs_0_.1) | copy-start | bytes 9437188
  19.6 55.6 %copy-start.2 = (bf16[2,2,152,256]{3,2,1,0:T(8,128)(2,1)S(1)}, bf16[2,2,152,256]{3,2,1,0:T(8,128)(2,1)}, u32[]{:S(2)}) copy-start(bf16[2,2,152,256]{3,2,1,0:T(8,128)(2,1)} %pad_maximum_fusion.refs_1_) | copy-start | bytes 933892
  60.6 12.7 %all-to-all-start.2 = ((f32[8,48,128]{2,1,0:T(8,128)}), f32[8,48,128]{2,1,0:T(8,128)}, u32[]{:S(2)}, u32[]{:S(2)}) async-start(f32[8,48,128]{2,1,0:T(8,128)} %broadcast_in_dim.13), calls=%async_computation.2 | async-start | bytes 393216 | tf_op jit(solution)/shard_map/all_to_all | solution.py:373
  67.3 158.4 %collective-permute-start.8 = (bf16[2,24,128,256]{3,2,1,0:T(8,128)(2,1)S(1)}, bf16[2,24,128,256]{3,2,1,0:T(8,128)(2,1)}, u32[]{:S(2)}, u32[]{:S(2)}) collective-permute-start(bf16[2,24,128,256]{3,2,1,0:T(8,128)(2,1)S(1)} %copy-done), channel_id=1, source_target_pairs={{0,3},{1,2},{2,1},{3,0},{4,7},{5,6},{6,5},{7,4},{8,11},{9,10},{10,... | collective-permute-start | bytes 9437192 | tf_op jit(solution)/shard_map/ppermute | solution.py:361
  73.3 167.6 %collective-permute-start.6 = (bf16[2,24,128,256]{3,2,1,0:T(8,128)(2,1)}, bf16[2,24,128,256]{3,2,1,0:T(8,128)(2,1)}, u32[]{:S(2)}, u32[]{:S(2)}) collective-permute-start(bf16[2,24,128,256]{3,2,1,0:T(8,128)(2,1)} %collective-permute-done.4.refs_0_), channel_id=1, source_target_pairs={{0,3},{1,2},{2,1},{3,0},{4,7},{5,6},{6,5},{7,4},{8,11},{9,10},{10,... | collective-permute-start | bytes 9437192 | tf_op jit(solution)/shard_map/ppermute | solution.py:361
  75.2 19.6 %collective-permute-start.5 = (bf16[2,2,152,256]{3,2,1,0:T(8,128)(2,1)S(1)}, bf16[2,2,152,256]{3,2,1,0:T(8,128)(2,1)}, u32[]{:S(2)}, u32[]{:S(2)}) collective-permute-start(bf16[2,2,152,256]{3,2,1,0:T(8,128)(2,1)S(1)} %copy-done.2), channel_id=1, source_target_pairs={{0,1},{1,0},{2,3},{3,2},{4,5},{5,4},{6,7},{7,6},{8,9},{9,8},{10,11... | collective-permute-start | bytes 933896 | tf_op jit(solution)/shard_map/ppermute | solution.py:361
  93.7 12.8 %collective-permute-start.10 = (f32[384,128]{1,0:T(8,128)}, f32[384,128]{1,0:T(8,128)}, u32[]{:S(2)}, u32[]{:S(2)}) collective-permute-start(f32[384,128]{1,0:T(8,128)} %shard_map.21.own_ref), channel_id=1, source_target_pairs={{0,1},{1,0},{2,3},{3,2},{4,5},{5,4},{6,7},{7,6},{8,9},{9,8},{10,11... | collective-permute-start | bytes 589832 | tf_op jit(solution)/shard_map/ppermute | solution.py:361
  162.2 93.7 %collective-permute-start.11 = (f32[640,128]{1,0:T(8,128)}, f32[640,128]{1,0:T(8,128)S(1)}, u32[]{:S(2)}, u32[]{:S(2)}) collective-permute-start(f32[640,128]{1,0:T(8,128)} %shard_map.23.own_ref), channel_id=1, source_target_pairs={{0,2},{1,3},{2,0},{3,1},{4,6},{5,7},{6,4},{7,5},{8,10},{9,11},{10,... | collective-permute-start | bytes 983048 | tf_op jit(solution)/shard_map/ppermute | solution.py:361
  162.5 63.2 %collective-permute-start.9 = (bf16[2,2,152,256]{3,2,1,0:T(8,128)(2,1)}, bf16[2,2,152,256]{3,2,1,0:T(8,128)(2,1)S(1)}, u32[]{:S(2)}, u32[]{:S(2)}) collective-permute-start(bf16[2,2,152,256]{3,2,1,0:T(8,128)(2,1)} %pad_maximum_fusion.refs_1_), channel_id=1, source_target_pairs={{0,3},{1,2},{2,1},{3,0},{4,7},{5,6},{6,5},{7,4},{8,11},{9,10},{10,... | collective-permute-start | bytes 933896 | tf_op jit(solution)/shard_map/ppermute | solution.py:361
  164.4 76.4 %collective-permute-start.7 = (bf16[2,2,152,256]{3,2,1,0:T(8,128)(2,1)}, bf16[2,2,152,256]{3,2,1,0:T(8,128)(2,1)S(1)}, u32[]{:S(2)}, u32[]{:S(2)}) collective-permute-start(bf16[2,2,152,256]{3,2,1,0:T(8,128)(2,1)} %pad_maximum_fusion.refs_1_), channel_id=1, source_target_pairs={{0,2},{1,3},{2,0},{3,1},{4,6},{5,7},{6,4},{7,5},{8,10},{9,11},{10,... | collective-permute-start | bytes 933896 | tf_op jit(solution)/shard_map/ppermute | solution.py:361
  225.7 0.7 copy-start.4
  240.8 0.7 copy-start.3
  255.9 0.7 copy-start.1
  271.1 10.5 %all-to-all-start.7 = ((f32[8,16,128]{2,1,0:T(8,128)}), f32[8,16,128]{2,1,0:T(8,128)S(1)}, u32[]{:S(2)}, u32[]{:S(2)}) async-start(f32[8,16,128]{2,1,0:T(8,128)} %broadcast_in_dim.16), calls=%async_computation.7 | async-start | bytes 131072 | tf_op jit(solution)/shard_map/all_to_all | solution.py:373
  282.2 10.1 %all-to-all-start.8 = ((f32[8,16,128]{2,1,0:T(8,128)}), f32[8,16,128]{2,1,0:T(8,128)S(1)}, u32[]{:S(2)}, u32[]{:S(2)}) async-start(f32[8,16,128]{2,1,0:T(8,128)} %broadcast_in_dim.17), calls=%async_computation.8 | async-start | bytes 131072 | tf_op jit(solution)/shard_map/all_to_all | solution.py:373
  292.3 0.6 copy-start.5

commit v2 on v1

--- a/solution.py
+++ b/solution.py
@@ -10,6 +10,7 @@
 BF = jnp.bfloat16
 HIGH = lax.Precision.HIGHEST
 ROWS = 4
+PAD = 8
 LIMIT = 56 * 2**20
 
 
@@ -207,40 +208,45 @@
     at = pl.program_id(0)
     _, height, wide, snaps = u_ref.shape
 
+    def place(c, line, row):
+        for h in range(snaps // 128):
+            field[c, line, h, PAD : PAD + wide, :] = row[:, h * 128 : (h + 1) * 128]
+
     @pl.when(at == 0)
     def _():
         sides[...] = halo_ref[:, :, wide:, :].astype(F32)
-        field[:, 0] = halo_ref[:, 0, :wide, :].astype(F32)
-        field[:, height + 1] = halo_ref[:, 1, :wide, :].astype(F32)
-        field[:, 1] = u_ref[:, 0].astype(F32)
+        for c in range(2):
+            place(c, 0, halo_ref[c, 0, :wide, :].astype(F32))
+            place(c, height + 1, halo_ref[c, 1, :wide, :].astype(F32))
+            place(c, 1, u_ref[c, 0].astype(F32))
         sums[...] = jnp.zeros_like(sums)
-
-    edge = lax.broadcasted_iota(jnp.int32, (wide, 128), 0)
 
     def one(r, carry):
         i = at * ROWS + r
 
         @pl.when(i + 1 < height)
         def _():
-            field[:, i + 2] = u_ref[:, i + 1].astype(F32)
-
-        for start in range(0, snaps, 128):
-            lanes = slice(start, start + 128)
+            for c in range(2):
+                place(c, i + 2, u_ref[c, i + 1].astype(F32))
+
+        for c in range(2):
+            for k, spot in ((0, PAD - 1), (1, PAD + wide)):
+                row = sides[c, k, pl.ds(i, 1), :]
+                for h in range(snaps // 128):
+                    field[c, i + 1, h, spot : spot + 1, :] = row[:, h * 128 : (h + 1) * 128]
+
+        for h in range(snaps // 128):
 
             def along_x(c):
-                return field[c, i + 2, :, lanes] - field[c, i, :, lanes]
+                return (
+                    field[c, i + 2, h, PAD : PAD + wide, :] - field[c, i, h, PAD : PAD + wide, :]
+                )
 
             def along_y(c):
-                here = field[c, i + 1, :, lanes]
-                back = jnp.where(
-                    edge == 0, sides[c, 0, pl.ds(i, 1), :][:, lanes], pltpu.roll(here, 1, 0)
+                return (
+                    field[c, i + 1, h, PAD + 1 : PAD + 1 + wide, :]
+                    - field[c, i + 1, h, PAD - 1 : PAD - 1 + wide, :]
                 )
-                ahead = jnp.where(
-                    edge == wide - 1,
-                    sides[c, 1, pl.ds(i, 1), :][:, lanes],
-                    pltpu.roll(here, wide - 1, 0),
-                )
-                return ahead - back
 
             strain_xx = along_x(0)
             strain_yy = along_y(1)
@@ -252,8 +258,8 @@
             span = pl.ds(pl.multiple_of(r * wide, wide), wide)
             for k, value in enumerate(values):
                 hi = value.astype(BF)
-                hi_ref[k, span, lanes] = hi
-                lo_ref[k, span, lanes] = (value - hi.astype(F32)).astype(BF)
+                hi_ref[k, span, h * 128 : (h + 1) * 128] = hi
+                lo_ref[k, span, h * 128 : (h + 1) * 128] = (value - hi.astype(F32)).astype(BF)
         return carry
 
     lax.fori_loop(0, ROWS, one, 0)
@@ -296,7 +302,7 @@
         out_specs=(part, part, pl.BlockSpec(shape, lambda i: (0, 0))),
         out_shape=(half, half, jax.ShapeDtypeStruct(shape, F32)),
         scratch_shapes=[
-            pltpu.VMEM((2, height + 2, wide, snaps), F32),
+            pltpu.VMEM((2, height + 2, snaps // 128, wide + 2 * PAD, 128), F32),
             pltpu.VMEM((2, 2, height, snaps), F32),
             pltpu.VMEM((snaps, max(count, 2) * snaps), F32),
         ],
@@ -376,7 +382,8 @@
 def all_sum(value):
     flat = value.reshape(-1, 128)
     part = scatter_sum(flat, "gx")
-    part = gathered(part, "gy").reshape(lax.axis_size("gy"), -1, 128).sum(0)
+    part = gathered(part, "gy")
+    part = part.reshape(lax.axis_size("gy"), -1, 128).sum(0)
     return gathered(part, "gx").reshape(value.shape)
 
 

time: 327 us -> 326 us (level)
  no operation moved by 1% of the time
where the time goes in v2:
time: 326 us; the launch traced here: 325 us
  Pallas kernels  125 us (38%)
  waiting for transfers between devices  79.8 us (24%)
  blocking collectives  73.1 us (22%)
  starting transfers between devices  36.3 us (11%)
  local copies, waits for them, and re-layouts  6.94 us (2%)
  other arithmetic  3.38 us (1%)
    ppermute x8, waiting for transfers between devices, swapped(): return lax.ppermute(value, 'cyc', pairs)  60.5 us
    pallas_call x4, Pallas kernels, features(): pl.pallas_call(lambda *refs: feature_kernel(count, *refs), grid=(height /...  50.2 us
    all_to_all x3, blocking collectives, gathered(): lax.all_to_all(copies.reshape(-1, value.shape[1]), axis, 0, 0, tiled=True)  41.4 us
    all_to_all x3, blocking collectives, scatter_sum(): parts = lax.all_to_all(value, axis, 0, 0, tiled=True)  31.7 us
    pallas_call x1, Pallas kernels, last_level(): pl.pallas_call(last_kernel, out_shape=jax.ShapeDtypeStruct((2 * pick.shap...  18.7 us
    pallas_call x1, Pallas kernels, next_level(): pl.pallas_call(level_kernel, out_shape=jax.ShapeDtypeStruct((2 * w + RANK...  18.5 us
    pallas_call x1, Pallas kernels, first_level(): pl.pallas_call(first_kernel, out_shape=jax.ShapeDtypeStruct((3 * RANK, RA...  18.1 us
    all_to_all x3, waiting for transfers between devices, gathered(): lax.all_to_all(copies.reshape(-1, value.shape[1]), axis, 0, 0, tiled=True)  15.4 us
  transfers between devices with their start and end apart: 15, of which 5 were waited for; matrix products, arithmetic and copies ran while one was open for 2% of the time, Pallas kernels for 28%

profile of v2, /device:TPU:1, one launch (start us, length us, event | category | flops | bytes accessed | tf_op | source)
XLA Modules:
  0.0 324.7 jit_solution(6108012937195098580)
XLA Ops:
  0.0 2.1 collective-permute-start.4
  2.1 1.0 slice_bitcast_fusion.1
  3.1 4.0 %collective-permute-start = (bf16[2,1,128,256]{3,2,0,1:T(8,128)(2,1)S(1)}, bf16[2,1,128,256]{3,2,0,1:T(8,128)(2,1)S(1)}, u32[]{:S(2)}, u32[]{:S(2)}) collective-permute-start(bf16[2,1,128,256]{3,2,0,1:T(8,128)(2,1)S(1)} %get-tuple-element.31), channel_id=1, source_target_pairs={{0,32},{32,64},{64,96},{96,128},{128,160},{160,192},{192,224},{1,3... | collective-permute-start | bytes 393224 | tf_op jit(solution)/shard_map/ppermute | solution.py:350
  7.1 1.1 fusion.1
  8.2 3.5 %collective-permute-start.1 = (bf16[2,24,1,256]{3,1,0,2:T(8,128)(2,1)S(1)}, bf16[2,24,1,256]{3,1,0,2:T(8,128)(2,1)S(1)}, u32[]{:S(2)}, u32[]{:S(2)}) collective-permute-start(bf16[2,24,1,256]{3,1,0,2:T(8,128)(2,1)S(1)} %copy.11), channel_id=1, source_target_pairs={{0,4},{4,8},{8,12},{12,16},{16,20},{20,24},{24,28},{1,5},{5,9},{9,... | collective-permute-start | bytes 73736 | tf_op jit(solution)/shard_map/ppermute | solution.py:350
  11.8 1.9 collective-permute-start.2
  13.7 1.3 collective-permute-start.3
  15.0 3.8 %collective-permute-done.3 = bf16[2,24,1,256]{3,1,0,2:T(8,128)(2,1)S(1)} collective-permute-done((bf16[2,24,1,256]{3,1,0,2:T(8,128)(2,1)S(1)}, bf16[2,24,1,256]{3,1,0,2:T(8,128)(2,1)S(1)}, u32[]{:S(2)}, u32[]{:S(2)}) %collective-permute-start.3) | collective-permute-done | bytes 24608 | tf_op jit(solution)/shard_map/ppermute | solution.py:353
  18.9 0.8 pad_maximum_fusion.refs_1_
  19.6 10.1 %shard_map.17 = (bf16[2,3072,256]{2,1,0:T(8,128)(2,1)}, bf16[2,3072,256]{2,1,0:T(8,128)(2,1)}, f32[384,128]{1,0:T(8,128)}) custom-call(bf16[2,24,128,256]{3,2,1,0:T(8,128)(2,1)} %refs_0_.1, bf16[2,2,152,256]{3,2,1,0:T(8,128)(2,1)} %pad_maximum_fusion.refs_1_), custom_call_target="tpu_custom_call" | custom-call | tf_op jit(solution)/shard_map/pallas_call | solution.py:298
  29.8 11.5 %all_to_all.69 = f32[8,48,128]{2,1,0:T(8,128)} all-to-all(f32[8,48,128]{2,1,0:T(8,128)} %bitcast.23), channel_id=1, replica_groups=mesh['gx'=8,'gy'=8,'cyc'=4] {'gx'}, dimensions={0} | all-to-all | bytes 393216 | tf_op jit(solution)/shard_map/all_to_all | solution.py:372
  41.2 0.9 reduce_sum.54
  42.2 16.6 %all_to_all.70 = f32[8,48,128]{2,1,0:T(8,128)} all-to-all(f32[8,48,128]{2,1,0:T(8,128)S(1)} %broadcast_in_dim.12), channel_id=1, replica_groups=mesh['gx'=8,'gy'=8,'cyc'=4] {'gy'}, dimensions={0} | all-to-all | bytes 393216 | tf_op jit(solution)/shard_map/all_to_all | solution.py:379
  58.7 0.9 reduce_sum.55
  59.7 0.7 broadcast_in_dim.13
  60.4 6.7 %all-to-all-start.2 = ((f32[8,48,128]{2,1,0:T(8,128)}), f32[8,48,128]{2,1,0:T(8,128)}, u32[]{:S(2)}, u32[]{:S(2)}) async-start(f32[8,48,128]{2,1,0:T(8,128)} %broadcast_in_dim.13), calls=%async_computation.2 | async-start | bytes 393216 | tf_op jit(solution)/shard_map/all_to_all | solution.py:379
  67.1 1.9 collective-permute-start.8
  69.0 4.1 %all-to-all-done.2 = f32[8,48,128]{2,1,0:T(8,128)} async-done(((f32[8,48,128]{2,1,0:T(8,128)}), f32[8,48,128]{2,1,0:T(8,128)}, u32[]{:S(2)}, u32[]{:S(2)}) %all-to-all-start.2) | async-done | bytes 196640 | tf_op jit(solution)/shard_map/all_to_all | solution.py:379
  73.1 1.9 collective-permute-start.6
  75.0 0.4 collective-permute-start.5
  75.4 18.1 %shard_map.21.own_ref = f32[384,128]{1,0:T(8,128)} custom-call(f32[384,128]{1,0:T(8,128)} %bitcast.7.g_ref), custom_call_target="tpu_custom_call" | custom-call | tf_op jit(solution)/shard_map/pallas_call | solution.py:134
  93.5 1.1 collective-permute-start.10
  94.6 11.6 %shard_map.18 = (bf16[2,3072,256]{2,1,0:T(8,128)(2,1)}, bf16[2,3072,256]{2,1,0:T(8,128)(2,1)}, f32[256,256]{1,0:T(8,128)}) custom-call(bf16[2,24,128,256]{3,2,1,0:T(8,128)(2,1)} %collective-permute-done.4.refs_0_, bf16[2,2,152,256]{3,2,1,0:T(8,128)(2,1)} %collective-permute-done.5.refs_1_, bf16[2,3072,256]{2,1,0:T(8,128)(2,1)} %get-tuple-element.18.refs_2_.refs_0_, ...), custom_call_target="tpu_custom_call" | custom-call | tf_op jit(solution)/shard_map/pallas_call | solution.py:298
  106.2 2.6 shard_map.22
  108.8 9.9 %all_to_all.71 = f32[8,16,128]{2,1,0:T(8,128)S(1)} all-to-all(f32[8,16,128]{2,1,0:T(8,128)} %bitcast.22), channel_id=1, replica_groups=mesh['gx'=8,'gy'=8,'cyc'=4] {'gx'}, dimensions={0} | all-to-all | bytes 131072 | tf_op jit(solution)/shard_map/all_to_all | solution.py:372
  118.7 14.7 %all_to_all.72 = f32[8,16,128]{2,1,0:T(8,128)S(1)} all-to-all(f32[8,16,128]{2,1,0:T(8,128)S(1)} %broadcast_in_dim.14), channel_id=1, replica_groups=mesh['gx'=8,'gy'=8,'cyc'=4] {'gy'}, dimensions={0} | all-to-all | bytes 131072 | tf_op jit(solution)/shard_map/all_to_all | solution.py:379
  133.5 10.1 %all_to_all.73 = f32[8,16,128]{2,1,0:T(8,128)} all-to-all(f32[8,16,128]{2,1,0:T(8,128)S(1)} %broadcast_in_dim.15), channel_id=1, replica_groups=mesh['gx'=8,'gy'=8,'cyc'=4] {'gx'}, dimensions={0} | all-to-all | bytes 131072 | tf_op jit(solution)/shard_map/all_to_all | solution.py:379
  143.6 18.5 %shard_map.23.own_ref = f32[640,128]{1,0:T(8,128)} custom-call(f32[384,128]{1,0:T(8,128)} %shard_map.21.own_ref, f32[128,128]{1,0:T(8,128)} %bitcast.20, f32[384,128]{1,0:T(8,128)} %collective-permute-done.10.far_ref), custom_call_target="tpu_custom_call" | custom-call | tf_op jit(solution)/shard_map/pallas_call | solution.py:158
  162.4 1.9 collective-permute-start.9
  164.3 0.7 collective-permute-start.7
  165.0 60.5 %collective-permute-done.9.refs_1_ = bf16[2,2,152,256]{3,2,1,0:T(8,128)(2,1)S(1)} collective-permute-done((bf16[2,2,152,256]{3,2,1,0:T(8,128)(2,1)}, bf16[2,2,152,256]{3,2,1,0:T(8,128)(2,1)S(1)}, u32[]{:S(2)}, u32[]{:S(2)}) %collective-permute-start.9) | collective-permute-done | bytes 311328 | tf_op jit(solution)/shard_map/ppermute | solution.py:367
  225.5 0.7 copy-done.4
  226.3 14.2 %shard_map.20 = (bf16[2,3072,256]{2,1,0:T(8,128)(2,1)}, bf16[2,3072,256]{2,1,0:T(8,128)(2,1)}, f32[256,512]{1,0:T(8,128)}) custom-call(bf16[2,24,128,256]{3,2,1,0:T(8,128)(2,1)} %collective-permute-done.8.refs_0_, bf16[2,2,152,256]{3,2,1,0:T(8,128)(2,1)} %copy-done.4, bf16[2,3072,256]{2,1,0:T(8,128)(2,1)} %get-tuple-element.18.refs_2_.refs_0_, ...), custom_call_target="tpu_custom_call" | custom-call | tf_op jit(solution)/shard_map/pallas_call | solution.py:298
  240.6 0.7 copy-done.3
  241.3 14.2 %shard_map.19 = (bf16[2,3072,256]{2,1,0:T(8,128)(2,1)}, bf16[2,3072,256]{2,1,0:T(8,128)(2,1)}, f32[256,512]{1,0:T(8,128)}) custom-call(bf16[2,24,128,256]{3,2,1,0:T(8,128)(2,1)} %collective-permute-done.6.refs_0_, bf16[2,2,152,256]{3,2,1,0:T(8,128)(2,1)} %copy-done.3, bf16[2,3072,256]{2,1,0:T(8,128)(2,1)} %get-tuple-element.18.refs_2_.refs_0_, ...), custom_call_target="tpu_custom_call" | custom-call | tf_op jit(solution)/shard_map/pallas_call | solution.py:298
  255.5 0.7 copy-done.1
  256.2 3.4 %shard_map.24 = f32[128,128]{1,0:T(8,128)} custom-call(f32[640,128]{1,0:T(8,128)} %shard_map.23.own_ref, f32[640,128]{1,0:T(8,128)} %copy-done.1, f32[256,512]{1,0:T(8,128)} %get-tuple-element.29.refs_0_, f32[256,512]{1,0:T(8,128)} %get-tuple-element.30.refs_1_), custom_call_target="tpu_custom_call" | custom-call | tf_op jit(solution)/shard_map/pallas_call | solution.py:200
  259.6 10.4 %all_to_all.74 = f32[8,16,128]{2,1,0:T(8,128)S(1)} all-to-all(f32[8,16,128]{2,1,0:T(8,128)} %bitcast.19), channel_id=1, replica_groups=mesh['gx'=8,'gy'=8,'cyc'=4] {'gx'}, dimensions={0} | all-to-all | bytes 131072 | tf_op jit(solution)/shard_map/all_to_all | solution.py:372
  270.0 0.6 broadcast_in_dim.16
  270.6 3.4 %all-to-all-start.7 = ((f32[8,16,128]{2,1,0:T(8,128)}), f32[8,16,128]{2,1,0:T(8,128)S(1)}, u32[]{:S(2)}, u32[]{:S(2)}) async-start(f32[8,16,128]{2,1,0:T(8,128)} %broadcast_in_dim.16), calls=%async_computation.7 | async-start | bytes 131072 | tf_op jit(solution)/shard_map/all_to_all | solution.py:379
  274.0 7.1 %all-to-all-done.7 = f32[8,16,128]{2,1,0:T(8,128)S(1)} async-done(((f32[8,16,128]{2,1,0:T(8,128)}), f32[8,16,128]{2,1,0:T(8,128)S(1)}, u32[]{:S(2)}, u32[]{:S(2)}) %all-to-all-start.7) | async-done | bytes 65568 | tf_op jit(solution)/shard_map/all_to_all | solution.py:379
  281.2 0.6 broadcast_in_dim.17
  281.8 5.2 %all-to-all-start.8 = ((f32[8,16,128]{2,1,0:T(8,128)}), f32[8,16,128]{2,1,0:T(8,128)S(1)}, u32[]{:S(2)}, u32[]{:S(2)}) async-start(f32[8,16,128]{2,1,0:T(8,128)} %broadcast_in_dim.17), calls=%async_computation.8 | async-start | bytes 131072 | tf_op jit(solution)/shard_map/all_to_all | solution.py:379
  287.0 0.7 fusion.pick_ref
  287.6 4.2 %all-to-all-done.8 = f32[8,16,128]{2,1,0:T(8,128)S(1)} async-done(((f32[8,16,128]{2,1,0:T(8,128)}), f32[8,16,128]{2,1,0:T(8,128)S(1)}, u32[]{:S(2)}, u32[]{:S(2)}) %all-to-all-start.8) | async-done | bytes 65568 | tf_op jit(solution)/shard_map/all_to_all | solution.py:379
  291.9 0.6 copy-done.5
  292.5 18.7 %shard_map.25.refs_8_ = bf16[64,1024]{1,0:T(8,128)(2,1)} custom-call(f32[640,128]{1,0:T(8,128)} %shard_map.23.own_ref, f32[128,128]{1,0:T(8,128)} %bitcast.21, f32[640,128]{1,0:T(8,128)} %copy-done.1, f32[32,128]{1,0:T(8,128)} %fusion.pick_ref), custom_call_target="tpu_custom_call" | custom-call | tf_op jit(solution)/shard_map/pallas_call | solution.py:180
  311.2 13.6 %shard_map.26 = f32[2,24,32,128]{3,2,1,0:T(8,128)} custom-call(bf16[2,3072,256]{2,1,0:T(8,128)(2,1)} %get-tuple-element.18.refs_2_.refs_0_, bf16[2,3072,256]{2,1,0:T(8,128)(2,1)} %get-tuple-element.19.refs_3_.refs_1_, bf16[2,3072,256]{2,1,0:T(8,128)(2,1)} %get-tuple-element.20.refs_4_.refs_2_, bf16[2,3072,256]{2,1,0:T(8,128)(2,1)} %get-tuple-element.21.refs_5_.refs_3_, ...), custom_call_target="tpu_custom_call" | custom-call | tf_op jit(solution)/shard_map/pallas_call | solution.py:335
  (31 shorter events, 0.5 us)
Async XLA Ops:
  0.0 73.1 %collective-permute-start.4 = (bf16[2,24,128,256]{3,2,1,0:T(8,128)(2,1)}, bf16[2,24,128,256]{3,2,1,0:T(8,128)(2,1)}, u32[]{:S(2)}, u32[]{:S(2)}) collective-permute-start(bf16[2,24,128,256]{3,2,1,0:T(8,128)(2,1)} %refs_0_.1), channel_id=1, source_target_pairs={{0,1},{1,0},{2,3},{3,2},{4,5},{5,4},{6,7},{7,6},{8,9},{9,8},{10,11... | collective-permute-start | bytes 9437192 | tf_op jit(solution)/shard_map/ppermute | solution.py:367
  3.1 11.9 %collective-permute-start = (bf16[2,1,128,256]{3,2,0,1:T(8,128)(2,1)S(1)}, bf16[2,1,128,256]{3,2,0,1:T(8,128)(2,1)S(1)}, u32[]{:S(2)}, u32[]{:S(2)}) collective-permute-start(bf16[2,1,128,256]{3,2,0,1:T(8,128)(2,1)S(1)} %get-tuple-element.31), channel_id=1, source_target_pairs={{0,32},{32,64},{64,96},{96,128},{128,160},{160,192},{192,224},{1,3... | collective-permute-start | bytes 393224 | tf_op jit(solution)/shard_map/ppermute | solution.py:350
  8.2 6.8 %collective-permute-start.1 = (bf16[2,24,1,256]{3,1,0,2:T(8,128)(2,1)S(1)}, bf16[2,24,1,256]{3,1,0,2:T(8,128)(2,1)S(1)}, u32[]{:S(2)}, u32[]{:S(2)}) collective-permute-start(bf16[2,24,1,256]{3,1,0,2:T(8,128)(2,1)S(1)} %copy.11), channel_id=1, source_target_pairs={{0,4},{4,8},{8,12},{12,16},{16,20},{20,24},{24,28},{1,5},{5,9},{9,... | collective-permute-start | bytes 73736 | tf_op jit(solution)/shard_map/ppermute | solution.py:350
  11.8 7.1 %collective-permute-start.2 = (bf16[2,1,128,256]{3,2,0,1:T(8,128)(2,1)S(1)}, bf16[2,1,128,256]{3,2,0,1:T(8,128)(2,1)S(1)}, u32[]{:S(2)}, u32[]{:S(2)}) collective-permute-start(bf16[2,1,128,256]{3,2,0,1:T(8,128)(2,1)S(1)} %get-tuple-element.32), channel_id=1, source_target_pairs={{32,0},{64,32},{96,64},{128,96},{160,128},{192,160},{224,192},{33,... | collective-permute-start | bytes 393224 | tf_op jit(solution)/shard_map/ppermute | solution.py:353
  13.7 5.2 %collective-permute-start.3 = (bf16[2,24,1,256]{3,1,0,2:T(8,128)(2,1)S(1)}, bf16[2,24,1,256]{3,1,0,2:T(8,128)(2,1)S(1)}, u32[]{:S(2)}, u32[]{:S(2)}) collective-permute-start(bf16[2,24,1,256]{3,1,0,2:T(8,128)(2,1)S(1)} %copy.13), channel_id=1, source_target_pairs={{4,0},{8,4},{12,8},{16,12},{20,16},{24,20},{28,24},{5,1},{9,5},{13... | collective-permute-start | bytes 73736 | tf_op jit(solution)/shard_map/ppermute | solution.py:353
  18.9 48.2 %copy-start = (bf16[2,24,128,256]{3,2,1,0:T(8,128)(2,1)S(1)}, bf16[2,24,128,256]{3,2,1,0:T(8,128)(2,1)}, u32[]{:S(2)}) copy-start(bf16[2,24,128,256]{3,2,1,0:T(8,128)(2,1)} %refs_0_.1) | copy-start | bytes 9437188
  19.6 55.4 %copy-start.2 = (bf16[2,2,152,256]{3,2,1,0:T(8,128)(2,1)S(1)}, bf16[2,2,152,256]{3,2,1,0:T(8,128)(2,1)}, u32[]{:S(2)}) copy-start(bf16[2,2,152,256]{3,2,1,0:T(8,128)(2,1)} %pad_maximum_fusion.refs_1_) | copy-start | bytes 933892
  60.4 12.7 %all-to-all-start.2 = ((f32[8,48,128]{2,1,0:T(8,128)}), f32[8,48,128]{2,1,0:T(8,128)}, u32[]{:S(2)}, u32[]{:S(2)}) async-start(f32[8,48,128]{2,1,0:T(8,128)} %broadcast_in_dim.13), calls=%async_computation.2 | async-start | bytes 393216 | tf_op jit(solution)/shard_map/all_to_all | solution.py:379
  67.1 158.4 %collective-permute-start.8 = (bf16[2,24,128,256]{3,2,1,0:T(8,128)(2,1)S(1)}, bf16[2,24,128,256]{3,2,1,0:T(8,128)(2,1)}, u32[]{:S(2)}, u32[]{:S(2)}) collective-permute-start(bf16[2,24,128,256]{3,2,1,0:T(8,128)(2,1)S(1)} %copy-done), channel_id=1, source_target_pairs={{0,3},{1,2},{2,1},{3,0},{4,7},{5,6},{6,5},{7,4},{8,11},{9,10},{10,... | collective-permute-start | bytes 9437192 | tf_op jit(solution)/shard_map/ppermute | solution.py:367
  73.1 167.4 %collective-permute-start.6 = (bf16[2,24,128,256]{3,2,1,0:T(8,128)(2,1)}, bf16[2,24,128,256]{3,2,1,0:T(8,128)(2,1)}, u32[]{:S(2)}, u32[]{:S(2)}) collective-permute-start(bf16[2,24,128,256]{3,2,1,0:T(8,128)(2,1)} %collective-permute-done.4.refs_0_), channel_id=1, source_target_pairs={{0,3},{1,2},{2,1},{3,0},{4,7},{5,6},{6,5},{7,4},{8,11},{9,10},{10,... | collective-permute-start | bytes 9437192 | tf_op jit(solution)/shard_map/ppermute | solution.py:367
  75.0 19.6 %collective-permute-start.5 = (bf16[2,2,152,256]{3,2,1,0:T(8,128)(2,1)S(1)}, bf16[2,2,152,256]{3,2,1,0:T(8,128)(2,1)}, u32[]{:S(2)}, u32[]{:S(2)}) collective-permute-start(bf16[2,2,152,256]{3,2,1,0:T(8,128)(2,1)S(1)} %copy-done.2), channel_id=1, source_target_pairs={{0,1},{1,0},{2,3},{3,2},{4,5},{5,4},{6,7},{7,6},{8,9},{9,8},{10,11... | collective-permute-start | bytes 933896 | tf_op jit(solution)/shard_map/ppermute | solution.py:367
  93.5 12.7 %collective-permute-start.10 = (f32[384,128]{1,0:T(8,128)}, f32[384,128]{1,0:T(8,128)}, u32[]{:S(2)}, u32[]{:S(2)}) collective-permute-start(f32[384,128]{1,0:T(8,128)} %shard_map.21.own_ref), channel_id=1, source_target_pairs={{0,1},{1,0},{2,3},{3,2},{4,5},{5,4},{6,7},{7,6},{8,9},{9,8},{10,11... | collective-permute-start | bytes 589832 | tf_op jit(solution)/shard_map/ppermute | solution.py:367
  162.1 93.4 %collective-permute-start.11 = (f32[640,128]{1,0:T(8,128)}, f32[640,128]{1,0:T(8,128)S(1)}, u32[]{:S(2)}, u32[]{:S(2)}) collective-permute-start(f32[640,128]{1,0:T(8,128)} %shard_map.23.own_ref), channel_id=1, source_target_pairs={{0,2},{1,3},{2,0},{3,1},{4,6},{5,7},{6,4},{7,5},{8,10},{9,11},{10,... | collective-permute-start | bytes 983048 | tf_op jit(solution)/shard_map/ppermute | solution.py:367
  162.4 63.1 %collective-permute-start.9 = (bf16[2,2,152,256]{3,2,1,0:T(8,128)(2,1)}, bf16[2,2,152,256]{3,2,1,0:T(8,128)(2,1)S(1)}, u32[]{:S(2)}, u32[]{:S(2)}) collective-permute-start(bf16[2,2,152,256]{3,2,1,0:T(8,128)(2,1)} %pad_maximum_fusion.refs_1_), channel_id=1, source_target_pairs={{0,3},{1,2},{2,1},{3,0},{4,7},{5,6},{6,5},{7,4},{8,11},{9,10},{10,... | collective-permute-start | bytes 933896 | tf_op jit(solution)/shard_map/ppermute | solution.py:367
  164.3 76.2 %collective-permute-start.7 = (bf16[2,2,152,256]{3,2,1,0:T(8,128)(2,1)}, bf16[2,2,152,256]{3,2,1,0:T(8,128)(2,1)S(1)}, u32[]{:S(2)}, u32[]{:S(2)}) collective-permute-start(bf16[2,2,152,256]{3,2,1,0:T(8,128)(2,1)} %pad_maximum_fusion.refs_1_), channel_id=1, source_target_pairs={{0,2},{1,3},{2,0},{3,1},{4,6},{5,7},{6,4},{7,5},{8,10},{9,11},{10,... | collective-permute-start | bytes 933896 | tf_op jit(solution)/shard_map/ppermute | solution.py:367
  225.5 0.7 copy-start.4
  240.5 0.7 copy-start.3
  255.5 0.7 copy-start.1
  270.6 10.5 %all-to-all-start.7 = ((f32[8,16,128]{2,1,0:T(8,128)}), f32[8,16,128]{2,1,0:T(8,128)S(1)}, u32[]{:S(2)}, u32[]{:S(2)}) async-start(f32[8,16,128]{2,1,0:T(8,128)} %broadcast_in_dim.16), calls=%async_computation.7 | async-start | bytes 131072 | tf_op jit(solution)/shard_map/all_to_all | solution.py:379
  281.8 10.1 %all-to-all-start.8 = ((f32[8,16,128]{2,1,0:T(8,128)}), f32[8,16,128]{2,1,0:T(8,128)S(1)}, u32[]{:S(2)}, u32[]{:S(2)}) async-start(f32[8,16,128]{2,1,0:T(8,128)} %broadcast_in_dim.17), calls=%async_computation.8 | async-start | bytes 131072 | tf_op jit(solution)/shard_map/all_to_all | solution.py:379
  291.8 0.6 copy-start.5

commit v3 on v2

--- a/solution.py
+++ b/solution.py
@@ -167,19 +167,16 @@
     h = joined_gram(own_ref[w:], cross_ref[...], far_ref[w:])
     u = vectors_of(h, work, moved, found)
     share = pick_ref.shape[0]
-    for at, ref in ((0, own_ref), (1, far_ref)):
-        mine = mm(pick_ref[...], u[at * RANK : (at + 1) * RANK], 1, 1)
-        part = mm(mine, ref[:w], 1, 1)
-        top = part.astype(BF)
-        out_ref[:share, at * w : (at + 1) * w] = top
-        out_ref[share:, at * w : (at + 1) * w] = (part - top.astype(F32)).astype(BF)
+    part = mm(pick_ref[...], u, 1, 1)
+    top = part.astype(BF)
+    out_ref[:share] = top
+    out_ref[share:] = (part - top.astype(F32)).astype(BF)
 
 
 def last_level(own, cross, far, pick):
-    w = own.shape[0] - RANK
     return pl.pallas_call(
         last_kernel,
-        out_shape=jax.ShapeDtypeStruct((2 * pick.shape[0], 2 * w), BF),
+        out_shape=jax.ShapeDtypeStruct((2 * pick.shape[0], 2 * RANK), BF),
         scratch_shapes=scratch(),
     )(own, cross, far, pick)
 
@@ -197,16 +194,17 @@
 
 
 def project(own, far, blocks):
-    return pl.pallas_call(project_kernel, out_shape=jax.ShapeDtypeStruct((RANK, RANK), F32))(
-        own, far, *blocks
-    )
-
-
-def feature_kernel(count, u_ref, halo_ref, *refs):
+    return pl.pallas_call(
+        project_kernel,
+        out_shape=jax.ShapeDtypeStruct((RANK, RANK), F32),
+    )(own, far, *blocks)
+
+
+def feature_kernel(count, height, first_ref, u_ref, halo_ref, *refs):
     left = refs[: 2 * count]
     hi_ref, lo_ref, gram_ref, field, sides, sums = refs[2 * count :]
     at = pl.program_id(0)
-    _, height, wide, snaps = u_ref.shape
+    _, _, wide, snaps = u_ref.shape
 
     def place(c, line, row):
         for h in range(snaps // 128):
@@ -218,16 +216,22 @@
         for c in range(2):
             place(c, 0, halo_ref[c, 0, :wide, :].astype(F32))
             place(c, height + 1, halo_ref[c, 1, :wide, :].astype(F32))
-            place(c, 1, u_ref[c, 0].astype(F32))
+            for r in range(ROWS):
+                place(c, 1 + r, first_ref[c, r].astype(F32))
         sums[...] = jnp.zeros_like(sums)
+
+    @pl.when((at + 1) * ROWS < height)
+    def _():
+        for c in range(2):
+            place(c, (at + 1) * ROWS + 1, u_ref[c, 0].astype(F32))
 
     def one(r, carry):
         i = at * ROWS + r
 
-        @pl.when(i + 1 < height)
+        @pl.when((r > 0) & (i + ROWS < height))
         def _():
             for c in range(2):
-                place(c, i + 2, u_ref[c, i + 1].astype(F32))
+                place(c, i + ROWS + 1, u_ref[c, r].astype(F32))
 
         for c in range(2):
             for k, spot in ((0, PAD - 1), (1, PAD + wide)):
@@ -291,14 +295,20 @@
 def features(u, halo, lefts):
     _, height, wide, snaps = u.shape
     count = len(lefts)
+    last = height // ROWS - 1
     full = lambda array: pl.BlockSpec(array.shape, lambda i: (0,) * array.ndim)
     part = pl.BlockSpec((2, ROWS * wide, snaps), lambda i: (0, i, 0))
     half = jax.ShapeDtypeStruct((2, height * wide, snaps), BF)
     shape = (snaps, count * snaps) if count else (3 * RANK, RANK)
     hi, lo, gram = pl.pallas_call(
-        lambda *refs: feature_kernel(count, *refs),
+        lambda *refs: feature_kernel(count, height, *refs),
         grid=(height // ROWS,),
-        in_specs=[full(u), full(halo)] + [part] * (2 * count),
+        in_specs=[
+            pl.BlockSpec((2, ROWS, wide, snaps), lambda i: (0, 0, 0, 0)),
+            pl.BlockSpec((2, ROWS, wide, snaps), lambda i: (0, jnp.minimum(i + 1, last), 0, 0)),
+            full(halo),
+        ]
+        + [part] * (2 * count),
         out_specs=(part, part, pl.BlockSpec(shape, lambda i: (0, 0))),
         out_shape=(half, half, jax.ShapeDtypeStruct(shape, F32)),
         scratch_shapes=[
@@ -307,40 +317,69 @@
             pltpu.VMEM((snaps, max(count, 2) * snaps), F32),
         ],
         compiler_params=pltpu.CompilerParams(vmem_limit_bytes=LIMIT),
-    )(u, halo, *[array for pair in lefts for array in pair])
+    )(u, u, halo, *[array for pair in lefts for array in pair])
     return (hi, lo), gram
 
 
-def finish_kernel(*refs):
+def mix_kernel(*refs):
     *halves, w_ref, o_ref = refs
     groups = len(halves) // 2
-    snaps = w_ref.shape[1] // groups
+    snaps = halves[0].shape[2]
+    total = jnp.zeros(o_ref.shape[1:], F32)
+    for g in range(groups):
+        w = w_ref[g * snaps : (g + 1) * snaps]
+        top = w.astype(BF)
+        low = (w - top.astype(F32)).astype(BF)
+        hi = halves[2 * g][0]
+        both = fast(hi, jnp.concatenate([top, low], axis=1), 1, 0)
+        total += both[:, :RANK] + both[:, RANK:]
+        total += fast(halves[2 * g + 1][0], top, 1, 0)
+    o_ref[0] = total
+
+
+def mix(pairs, vectors):
+    chunk = 1024
+    _, nodes, snaps = pairs[0][0].shape
+    part = pl.BlockSpec((1, chunk, snaps), lambda k, i: (k, i, 0))
+    return pl.pallas_call(
+        mix_kernel,
+        grid=(2, nodes // chunk),
+        in_specs=[part] * (2 * len(pairs))
+        + [pl.BlockSpec(vectors.shape, lambda k, i: (0, 0))],
+        out_specs=pl.BlockSpec((1, chunk, RANK), lambda k, i: (k, i, 0)),
+        out_shape=jax.ShapeDtypeStruct((2, nodes, RANK), F32),
+        compiler_params=pltpu.CompilerParams(vmem_limit_bytes=LIMIT),
+    )(*[array for pair in pairs for array in pair], vectors)
+
+
+def finish_kernel(first_ref, second_ref, w_ref, o_ref):
     share = w_ref.shape[0] // 2
     wide = o_ref.shape[-1]
-    total = jnp.zeros((share, halves[0].shape[1]), F32)
-    for g in range(groups):
-        w = w_ref[:, g * snaps : (g + 1) * snaps]
-        both = fast(w, halves[2 * g][0], 1, 1)
+    total = jnp.zeros((share, first_ref.shape[1]), F32)
+    for g, ref in enumerate((first_ref, second_ref)):
+        w = w_ref[:, g * RANK : (g + 1) * RANK]
+        value = ref[0]
+        hi = value.astype(BF)
+        lo = (value - hi.astype(F32)).astype(BF)
+        both = fast(w, hi, 1, 1)
         total += both[:share] + both[share:]
-        total += fast(w[:share], halves[2 * g + 1][0], 1, 1)
+        total += fast(w[:share], lo, 1, 1)
     for r in range(o_ref.shape[1]):
         o_ref[0, r] = total[:, r * wide : (r + 1) * wide]
 
 
-def finish(pairs, weights, height, wide):
+def finish(first, second, weights, height, wide):
     rows = 8
-    _, _, snaps = pairs[0][0].shape
     share = weights.shape[0] // 2
-    part = pl.BlockSpec((1, rows * wide, snaps), lambda k, i: (k, i, 0))
+    part = pl.BlockSpec((1, rows * wide, RANK), lambda k, i: (k, i, 0))
     return pl.pallas_call(
         finish_kernel,
         grid=(2, height // rows),
-        in_specs=[part] * (2 * len(pairs))
-        + [pl.BlockSpec(weights.shape, lambda k, i: (0, 0))],
+        in_specs=[part, part, pl.BlockSpec(weights.shape, lambda k, i: (0, 0))],
         out_specs=pl.BlockSpec((1, rows, share, wide), lambda k, i: (k, i, 0, 0)),
         out_shape=jax.ShapeDtypeStruct((2, height, share, wide), F32),
         compiler_params=pltpu.CompilerParams(vmem_limit_bytes=LIMIT),
-    )(*[array for pair in pairs for array in pair], weights)
+    )(first, second, weights)
 
 
 def edges(block, axis, dim):
@@ -410,8 +449,10 @@
     column = lax.axis_index("cyc") * share + jnp.arange(share)
     pick = (column[:, None] == jnp.arange(RANK)[None, :]).astype(F32)
     total = all_sum(project(level1, other1, [cross2, cross3]))
+    first = mix([own, pair], level1[: 4 * RANK])
+    second = mix([third, fourth], other1[: 4 * RANK])
     weights = last_level(level1, total, other1, pick)
-    result = finish([own, pair, third, fourth], weights, height, wide)
+    result = finish(first, second, weights, height, wide)
     return result.transpose(0, 1, 3, 2)
 
 

time: 326 us -> 334 us (1.025)
  Pallas kernels: 125 us -> 135 us
  waiting for transfers between devices: 79.8 us -> 75.8 us
    pallas_call x5 -> x7, Pallas kernels: 63.8 us -> 74.3 us  [the longest x4 49 us: features(): pl.pallas_call(lambda *refs: feature_kernel(count, height, *refs), grid=(...]
    all_to_all x3, waiting for transfers between devices: 15.4 us -> 11.2 us  [gathered(): lax.all_to_all(copies.reshape(-1, value.shape[1]), axis, 0, 0, tiled=True)]
  transfers between devices with their start and end apart: 15 -> 15, of which waited for: 5 -> 4; matrix products, arithmetic and copies ran while one was open for 2% -> 2% of each run, Pallas kernels for 28% -> 32%
where the time goes in v3:
time: 334 us; the launch traced here: 332 us
  Pallas kernels  135 us (40%)
  waiting for transfers between devices  75.8 us (23%)
  blocking collectives  73.2 us (22%)
  starting transfers between devices  36.3 us (11%)
  local copies, waits for them, and re-layouts  8.36 us (3%)
  other arithmetic  3.38 us (1%)
    ppermute x8, waiting for transfers between devices, swapped(): return lax.ppermute(value, 'cyc', pairs)  60.7 us
    pallas_call x4, Pallas kernels, features(): pl.pallas_call(lambda *refs: feature_kernel(count, height, *refs), grid=(...  49 us
    all_to_all x3, blocking collectives, gathered(): lax.all_to_all(copies.reshape(-1, value.shape[1]), axis, 0, 0, tiled=True)  41.5 us
    all_to_all x3, blocking collectives, scatter_sum(): parts = lax.all_to_all(value, axis, 0, 0, tiled=True)  31.7 us
    pallas_call x2, Pallas kernels, mix(): pl.pallas_call(mix_kernel, grid=(2, nodes // chunk), in_specs=[part] * (2...  18.8 us
    pallas_call x1, Pallas kernels, next_level(): pl.pallas_call(level_kernel, out_shape=jax.ShapeDtypeStruct((2 * w + RANK...  18.5 us
    pallas_call x1, Pallas kernels, first_level(): pl.pallas_call(first_kernel, out_shape=jax.ShapeDtypeStruct((3 * RANK, RA...  18.1 us
    pallas_call x1, Pallas kernels, last_level(): pl.pallas_call(last_kernel, out_shape=jax.ShapeDtypeStruct((2 * pick.shap...  17.7 us
  transfers between devices with their start and end apart: 15, of which 4 were waited for; matrix products, arithmetic and copies ran while one was open for 2% of the time, Pallas kernels for 32%

profile of v3, /device:TPU:1, one launch (start us, length us, event | category | flops | bytes accessed | tf_op | source)
XLA Modules:
  0.0 331.9 jit_solution(9384279747451819535)
XLA Ops:
  0.0 2.1 collective-permute-start.4
  2.1 1.0 slice_bitcast_fusion.1
  3.1 4.0 %collective-permute-start = (bf16[2,1,128,256]{3,2,0,1:T(8,128)(2,1)S(1)}, bf16[2,1,128,256]{3,2,0,1:T(8,128)(2,1)S(1)}, u32[]{:S(2)}, u32[]{:S(2)}) collective-permute-start(bf16[2,1,128,256]{3,2,0,1:T(8,128)(2,1)S(1)} %get-tuple-element.31), channel_id=1, source_target_pairs={{0,32},{32,64},{64,96},{96,128},{128,160},{160,192},{192,224},{1,3... | collective-permute-start | bytes 393224 | tf_op jit(solution)/shard_map/ppermute | solution.py:389
  7.1 1.1 fusion.1
  8.2 3.5 %collective-permute-start.1 = (bf16[2,24,1,256]{3,1,0,2:T(8,128)(2,1)S(1)}, bf16[2,24,1,256]{3,1,0,2:T(8,128)(2,1)S(1)}, u32[]{:S(2)}, u32[]{:S(2)}) collective-permute-start(bf16[2,24,1,256]{3,1,0,2:T(8,128)(2,1)S(1)} %copy.11), channel_id=1, source_target_pairs={{0,4},{4,8},{8,12},{12,16},{16,20},{20,24},{24,28},{1,5},{5,9},{9,... | collective-permute-start | bytes 73736 | tf_op jit(solution)/shard_map/ppermute | solution.py:389
  11.8 1.9 collective-permute-start.2
  13.7 1.3 collective-permute-start.3
  15.0 3.8 %collective-permute-done.3 = bf16[2,24,1,256]{3,1,0,2:T(8,128)(2,1)S(1)} collective-permute-done((bf16[2,24,1,256]{3,1,0,2:T(8,128)(2,1)S(1)}, bf16[2,24,1,256]{3,1,0,2:T(8,128)(2,1)S(1)}, u32[]{:S(2)}, u32[]{:S(2)}) %collective-permute-start.3) | collective-permute-done | bytes 24608 | tf_op jit(solution)/shard_map/ppermute | solution.py:392
  18.9 0.8 pad_maximum_fusion.refs_2_
  19.6 10.0 %shard_map.17 = (bf16[2,3072,256]{2,1,0:T(8,128)(2,1)}, bf16[2,3072,256]{2,1,0:T(8,128)(2,1)}, f32[384,128]{1,0:T(8,128)}) custom-call(bf16[2,24,128,256]{3,2,1,0:T(8,128)(2,1)} %refs_1_.1, bf16[2,24,128,256]{3,2,1,0:T(8,128)(2,1)} %refs_1_.1, bf16[2,2,152,256]{3,2,1,0:T(8,128)(2,1)} %pad_maximum_fusion.refs_2_), custom_call_target="tpu_custom_call" | custom-call | tf_op jit(solution)/shard_map/pallas_call | solution.py:303
  29.6 11.5 %all_to_all.69 = f32[8,48,128]{2,1,0:T(8,128)} all-to-all(f32[8,48,128]{2,1,0:T(8,128)} %bitcast.23), channel_id=1, replica_groups=mesh['gx'=8,'gy'=8,'cyc'=4] {'gx'}, dimensions={0} | all-to-all | bytes 393216 | tf_op jit(solution)/shard_map/all_to_all | solution.py:411
  41.1 0.9 reduce_sum.54
  42.1 16.6 %all_to_all.70 = f32[8,48,128]{2,1,0:T(8,128)} all-to-all(f32[8,48,128]{2,1,0:T(8,128)S(1)} %broadcast_in_dim.12), channel_id=1, replica_groups=mesh['gx'=8,'gy'=8,'cyc'=4] {'gy'}, dimensions={0} | all-to-all | bytes 393216 | tf_op jit(solution)/shard_map/all_to_all | solution.py:418
  58.6 0.9 reduce_sum.55
  59.6 0.7 broadcast_in_dim.13
  60.3 6.7 %all-to-all-start.2 = ((f32[8,48,128]{2,1,0:T(8,128)}), f32[8,48,128]{2,1,0:T(8,128)}, u32[]{:S(2)}, u32[]{:S(2)}) async-start(f32[8,48,128]{2,1,0:T(8,128)} %broadcast_in_dim.13), calls=%async_computation.2 | async-start | bytes 393216 | tf_op jit(solution)/shard_map/all_to_all | solution.py:418
  67.0 1.9 collective-permute-start.9
  68.9 4.1 %all-to-all-done.2 = f32[8,48,128]{2,1,0:T(8,128)} async-done(((f32[8,48,128]{2,1,0:T(8,128)}), f32[8,48,128]{2,1,0:T(8,128)}, u32[]{:S(2)}, u32[]{:S(2)}) %all-to-all-start.2) | async-done | bytes 196640 | tf_op jit(solution)/shard_map/all_to_all | solution.py:418
  73.0 1.9 collective-permute-start.7
  75.3 18.1 %shard_map.19.own_ref = f32[384,128]{1,0:T(8,128)} custom-call(f32[384,128]{1,0:T(8,128)} %bitcast.7.g_ref), custom_call_target="tpu_custom_call" | custom-call | tf_op jit(solution)/shard_map/pallas_call | solution.py:134
  93.4 1.1 collective-permute-start.6
  94.4 11.3 %shard_map.18 = (bf16[2,3072,256]{2,1,0:T(8,128)(2,1)}, bf16[2,3072,256]{2,1,0:T(8,128)(2,1)}, f32[256,256]{1,0:T(8,128)}) custom-call(bf16[2,24,128,256]{3,2,1,0:T(8,128)(2,1)} %collective-permute-done.4.refs_0_.refs_1_, bf16[2,24,128,256]{3,2,1,0:T(8,128)(2,1)} %collective-permute-done.4.refs_0_.refs_1_, ...), custom_call_target="tpu_custom_call" | custom-call | tf_op jit(solution)/shard_map/pallas_call | solution.py:303
  105.8 2.6 shard_map.20
  108.3 9.9 %all_to_all.71 = f32[8,16,128]{2,1,0:T(8,128)S(1)} all-to-all(f32[8,16,128]{2,1,0:T(8,128)} %bitcast.22), channel_id=1, replica_groups=mesh['gx'=8,'gy'=8,'cyc'=4] {'gx'}, dimensions={0} | all-to-all | bytes 131072 | tf_op jit(solution)/shard_map/all_to_all | solution.py:411
  118.3 14.8 %all_to_all.72 = f32[8,16,128]{2,1,0:T(8,128)S(1)} all-to-all(f32[8,16,128]{2,1,0:T(8,128)S(1)} %broadcast_in_dim.14), channel_id=1, replica_groups=mesh['gx'=8,'gy'=8,'cyc'=4] {'gy'}, dimensions={0} | all-to-all | bytes 131072 | tf_op jit(solution)/shard_map/all_to_all | solution.py:418
  133.1 10.1 %all_to_all.73 = f32[8,16,128]{2,1,0:T(8,128)} all-to-all(f32[8,16,128]{2,1,0:T(8,128)S(1)} %broadcast_in_dim.15), channel_id=1, replica_groups=mesh['gx'=8,'gy'=8,'cyc'=4] {'gx'}, dimensions={0} | all-to-all | bytes 131072 | tf_op jit(solution)/shard_map/all_to_all | solution.py:418
  143.2 18.5 %shard_map.21.own_ref = f32[640,128]{1,0:T(8,128)} custom-call(f32[384,128]{1,0:T(8,128)} %shard_map.19.own_ref, f32[128,128]{1,0:T(8,128)} %bitcast.21, f32[384,128]{1,0:T(8,128)} %collective-permute-done.6.far_ref), custom_call_target="tpu_custom_call" | custom-call | tf_op jit(solution)/shard_map/pallas_call | solution.py:158
  162.1 1.9 collective-permute-start.10
  164.0 0.7 collective-permute-start.8
  164.7 60.7 %collective-permute-done.10.refs_2_ = bf16[2,2,152,256]{3,2,1,0:T(8,128)(2,1)S(1)} collective-permute-done((bf16[2,2,152,256]{3,2,1,0:T(8,128)(2,1)}, bf16[2,2,152,256]{3,2,1,0:T(8,128)(2,1)S(1)}, u32[]{:S(2)}, u32[]{:S(2)}) %collective-permute-start.10) | collective-permute-done | bytes 311328 | tf_op jit(solution)/shard_map/ppermute | solution.py:406
  225.4 0.7 copy-done.6
  226.1 13.9 %shard_map.24 = (bf16[2,3072,256]{2,1,0:T(8,128)(2,1)}, bf16[2,3072,256]{2,1,0:T(8,128)(2,1)}, f32[256,512]{1,0:T(8,128)}) custom-call(bf16[2,24,128,256]{3,2,1,0:T(8,128)(2,1)} %collective-permute-done.9.refs_0_.refs_1_, bf16[2,24,128,256]{3,2,1,0:T(8,128)(2,1)} %collective-permute-done.9.refs_0_.refs_1_, bf16[2,2,152,256]{3,2,1,0:T(8,128)(2,1)} %copy-done.6, ...), custom_call_target="tpu_custom_call" | custom-call | tf_op jit(solution)/shard_map/pallas_call | solution.py:303
  240.1 0.7 copy-done.5
  240.8 13.9 %shard_map.23 = (bf16[2,3072,256]{2,1,0:T(8,128)(2,1)}, bf16[2,3072,256]{2,1,0:T(8,128)(2,1)}, f32[256,512]{1,0:T(8,128)}) custom-call(bf16[2,24,128,256]{3,2,1,0:T(8,128)(2,1)} %collective-permute-done.7.refs_0_.refs_1_, bf16[2,24,128,256]{3,2,1,0:T(8,128)(2,1)} %collective-permute-done.7.refs_0_.refs_1_, bf16[2,2,152,256]{3,2,1,0:T(8,128)(2,1)} %copy-done.5, ...), custom_call_target="tpu_custom_call" | custom-call | tf_op jit(solution)/shard_map/pallas_call | solution.py:303
  254.7 0.7 copy-done.2
  255.4 3.4 %shard_map.26 = f32[128,128]{1,0:T(8,128)} custom-call(f32[640,128]{1,0:T(8,128)} %shard_map.21.own_ref, f32[640,128]{1,0:T(8,128)} %copy-done.2, f32[256,512]{1,0:T(8,128)} %get-tuple-element.29.refs_0_, f32[256,512]{1,0:T(8,128)} %get-tuple-element.30.refs_1_), custom_call_target="tpu_custom_call" | custom-call | tf_op jit(solution)/shard_map/pallas_call | solution.py:197
  258.8 10.4 %all_to_all.74 = f32[8,16,128]{2,1,0:T(8,128)S(1)} all-to-all(f32[8,16,128]{2,1,0:T(8,128)} %bitcast.19), channel_id=1, replica_groups=mesh['gx'=8,'gy'=8,'cyc'=4] {'gx'}, dimensions={0} | all-to-all | bytes 131072 | tf_op jit(solution)/shard_map/all_to_all | solution.py:411
  269.2 0.6 broadcast_in_dim.16
  269.8 3.4 %all-to-all-start.7 = ((f32[8,16,128]{2,1,0:T(8,128)}), f32[8,16,128]{2,1,0:T(8,128)S(1)}, u32[]{:S(2)}, u32[]{:S(2)}) async-start(f32[8,16,128]{2,1,0:T(8,128)} %broadcast_in_dim.16), calls=%async_computation.7 | async-start | bytes 131072 | tf_op jit(solution)/shard_map/all_to_all | solution.py:418
  273.2 7.1 %all-to-all-done.7 = f32[8,16,128]{2,1,0:T(8,128)S(1)} async-done(((f32[8,16,128]{2,1,0:T(8,128)}), f32[8,16,128]{2,1,0:T(8,128)S(1)}, u32[]{:S(2)}, u32[]{:S(2)}) %all-to-all-start.7) | async-done | bytes 65568 | tf_op jit(solution)/shard_map/all_to_all | solution.py:418
  281.0 5.2 %all-to-all-start.8 = ((f32[8,16,128]{2,1,0:T(8,128)}), f32[8,16,128]{2,1,0:T(8,128)S(1)}, u32[]{:S(2)}, u32[]{:S(2)}) async-start(f32[8,16,128]{2,1,0:T(8,128)} %broadcast_in_dim.17), calls=%async_computation.8 | async-start | bytes 131072 | tf_op jit(solution)/shard_map/all_to_all | solution.py:418
  286.1 0.7 fusion.pick_ref
  286.8 0.7 slice.24.refs_4_
  287.5 9.4 %shard_map.22.first_ref = f32[2,3072,128]{2,1,0:T(8,128)} custom-call(bf16[2,3072,256]{2,1,0:T(8,128)(2,1)} %get-tuple-element.18.refs_3_.refs_0_, bf16[2,3072,256]{2,1,0:T(8,128)(2,1)} %get-tuple-element.19.refs_4_.refs_1_, bf16[2,3072,256]{2,1,0:T(8,128)(2,1)} %get-tuple-element.20.refs_2_.refs_5_, ...), custom_call_target="tpu_custom_call" | custom-call | tf_op jit(solution)/shard_map/pallas_call | solution.py:344
  296.9 0.7 slice.25.refs_4_
  297.7 9.4 %shard_map.25.second_ref = f32[2,3072,128]{2,1,0:T(8,128)} custom-call(bf16[2,3072,256]{2,1,0:T(8,128)(2,1)} %get-tuple-element.25.refs_0_, bf16[2,3072,256]{2,1,0:T(8,128)(2,1)} %get-tuple-element.26.refs_1_, bf16[2,3072,256]{2,1,0:T(8,128)(2,1)} %get-tuple-element.27.refs_2_, bf16[2,3072,256]{2,1,0:T(8,128)(2,1)} %get-tuple-element.28.refs_3_, ...), custom_call_target="tpu_custom_call" | custom-call | tf_op jit(solution)/shard_map/pallas_call | solution.py:344
  307.7 17.7 %shard_map.27.w_ref = bf16[64,256]{1,0:T(8,128)(2,1)} custom-call(f32[640,128]{1,0:T(8,128)} %shard_map.21.own_ref, f32[128,128]{1,0:T(8,128)} %bitcast.20, f32[640,128]{1,0:T(8,128)} %copy-done.2, f32[32,128]{1,0:T(8,128)} %fusion.pick_ref), custom_call_target="tpu_custom_call" | custom-call | tf_op jit(solution)/shard_map/pallas_call | solution.py:177
  325.4 6.5 %shard_map.28 = f32[2,24,32,128]{3,2,1,0:T(8,128)} custom-call(f32[2,3072,128]{2,1,0:T(8,128)} %shard_map.22.first_ref, f32[2,3072,128]{2,1,0:T(8,128)} %shard_map.25.second_ref, bf16[64,256]{1,0:T(8,128)(2,1)} %shard_map.27.w_ref), custom_call_target="tpu_custom_call" | custom-call | tf_op jit(solution)/shard_map/pallas_call | solution.py:375
  (39 shorter events, 2.2 us)
Async XLA Ops:
  0.0 73.0 %collective-permute-start.4 = (bf16[2,24,128,256]{3,2,1,0:T(8,128)(2,1)}, bf16[2,24,128,256]{3,2,1,0:T(8,128)(2,1)}, u32[]{:S(2)}, u32[]{:S(2)}) collective-permute-start(bf16[2,24,128,256]{3,2,1,0:T(8,128)(2,1)} %refs_1_.1), channel_id=1, source_target_pairs={{0,1},{1,0},{2,3},{3,2},{4,5},{5,4},{6,7},{7,6},{8,9},{9,8},{10,11... | collective-permute-start | bytes 9437192 | tf_op jit(solution)/shard_map/ppermute | solution.py:406
  3.1 11.9 %collective-permute-start = (bf16[2,1,128,256]{3,2,0,1:T(8,128)(2,1)S(1)}, bf16[2,1,128,256]{3,2,0,1:T(8,128)(2,1)S(1)}, u32[]{:S(2)}, u32[]{:S(2)}) collective-permute-start(bf16[2,1,128,256]{3,2,0,1:T(8,128)(2,1)S(1)} %get-tuple-element.31), channel_id=1, source_target_pairs={{0,32},{32,64},{64,96},{96,128},{128,160},{160,192},{192,224},{1,3... | collective-permute-start | bytes 393224 | tf_op jit(solution)/shard_map/ppermute | solution.py:389
  8.2 6.8 %collective-permute-start.1 = (bf16[2,24,1,256]{3,1,0,2:T(8,128)(2,1)S(1)}, bf16[2,24,1,256]{3,1,0,2:T(8,128)(2,1)S(1)}, u32[]{:S(2)}, u32[]{:S(2)}) collective-permute-start(bf16[2,24,1,256]{3,1,0,2:T(8,128)(2,1)S(1)} %copy.11), channel_id=1, source_target_pairs={{0,4},{4,8},{8,12},{12,16},{16,20},{20,24},{24,28},{1,5},{5,9},{9,... | collective-permute-start | bytes 73736 | tf_op jit(solution)/shard_map/ppermute | solution.py:389
  11.8 7.1 %collective-permute-start.2 = (bf16[2,1,128,256]{3,2,0,1:T(8,128)(2,1)S(1)}, bf16[2,1,128,256]{3,2,0,1:T(8,128)(2,1)S(1)}, u32[]{:S(2)}, u32[]{:S(2)}) collective-permute-start(bf16[2,1,128,256]{3,2,0,1:T(8,128)(2,1)S(1)} %get-tuple-element.32), channel_id=1, source_target_pairs={{32,0},{64,32},{96,64},{128,96},{160,128},{192,160},{224,192},{33,... | collective-permute-start | bytes 393224 | tf_op jit(solution)/shard_map/ppermute | solution.py:392
  13.7 5.2 %collective-permute-start.3 = (bf16[2,24,1,256]{3,1,0,2:T(8,128)(2,1)S(1)}, bf16[2,24,1,256]{3,1,0,2:T(8,128)(2,1)S(1)}, u32[]{:S(2)}, u32[]{:S(2)}) collective-permute-start(bf16[2,24,1,256]{3,1,0,2:T(8,128)(2,1)S(1)} %copy.13), channel_id=1, source_target_pairs={{4,0},{8,4},{12,8},{16,12},{20,16},{24,20},{28,24},{5,1},{9,5},{13... | collective-permute-start | bytes 73736 | tf_op jit(solution)/shard_map/ppermute | solution.py:392
  19.6 47.4 %copy-start = (bf16[2,24,128,256]{3,2,1,0:T(8,128)(2,1)S(1)}, bf16[2,24,128,256]{3,2,1,0:T(8,128)(2,1)}, u32[]{:S(2)}) copy-start(bf16[2,24,128,256]{3,2,1,0:T(8,128)(2,1)} %refs_1_.1) | copy-start | bytes 9437188
  19.6 55.2 %copy-start.4 = (bf16[2,2,152,256]{3,2,1,0:T(8,128)(2,1)S(1)}, bf16[2,2,152,256]{3,2,1,0:T(8,128)(2,1)}, u32[]{:S(2)}) copy-start(bf16[2,2,152,256]{3,2,1,0:T(8,128)(2,1)} %pad_maximum_fusion.refs_2_) | copy-start | bytes 933892
  60.3 12.7 %all-to-all-start.2 = ((f32[8,48,128]{2,1,0:T(8,128)}), f32[8,48,128]{2,1,0:T(8,128)}, u32[]{:S(2)}, u32[]{:S(2)}) async-start(f32[8,48,128]{2,1,0:T(8,128)} %broadcast_in_dim.13), calls=%async_computation.2 | async-start | bytes 393216 | tf_op jit(solution)/shard_map/all_to_all | solution.py:418
  67.0 158.4 %collective-permute-start.9 = (bf16[2,24,128,256]{3,2,1,0:T(8,128)(2,1)S(1)}, bf16[2,24,128,256]{3,2,1,0:T(8,128)(2,1)}, u32[]{:S(2)}, u32[]{:S(2)}) collective-permute-start(bf16[2,24,128,256]{3,2,1,0:T(8,128)(2,1)S(1)} %copy-done), channel_id=1, source_target_pairs={{0,3},{1,2},{2,1},{3,0},{4,7},{5,6},{6,5},{7,4},{8,11},{9,10},{10,... | collective-permute-start | bytes 9437192 | tf_op jit(solution)/shard_map/ppermute | solution.py:406
  73.0 167.1 %collective-permute-start.7 = (bf16[2,24,128,256]{3,2,1,0:T(8,128)(2,1)}, bf16[2,24,128,256]{3,2,1,0:T(8,128)(2,1)}, u32[]{:S(2)}, u32[]{:S(2)}) collective-permute-start(bf16[2,24,128,256]{3,2,1,0:T(8,128)(2,1)} %collective-permute-done.4.refs_0_.refs_1_), channel_id=1, source_target_pairs={{0,3},{1,2},{2,1},{3,0},{4,7},{5,6},{6,5},{7,4},{8,11},{9,10},{10,... | collective-permute-start | bytes 9437192 | tf_op jit(solution)/shard_map/ppermute | solution.py:406
  74.9 19.6 %collective-permute-start.5 = (bf16[2,2,152,256]{3,2,1,0:T(8,128)(2,1)S(1)}, bf16[2,2,152,256]{3,2,1,0:T(8,128)(2,1)}, u32[]{:S(2)}, u32[]{:S(2)}) collective-permute-start(bf16[2,2,152,256]{3,2,1,0:T(8,128)(2,1)S(1)} %copy-done.4), channel_id=1, source_target_pairs={{0,1},{1,0},{2,3},{3,2},{4,5},{5,4},{6,7},{7,6},{8,9},{9,8},{10,11... | collective-permute-start | bytes 933896 | tf_op jit(solution)/shard_map/ppermute | solution.py:406
  93.4 12.4 %collective-permute-start.6 = (f32[384,128]{1,0:T(8,128)}, f32[384,128]{1,0:T(8,128)}, u32[]{:S(2)}, u32[]{:S(2)}) collective-permute-start(f32[384,128]{1,0:T(8,128)} %shard_map.19.own_ref), channel_id=1, source_target_pairs={{0,1},{1,0},{2,3},{3,2},{4,5},{5,4},{6,7},{7,6},{8,9},{9,8},{10,11... | collective-permute-start | bytes 589832 | tf_op jit(solution)/shard_map/ppermute | solution.py:406
  161.7 92.9 %collective-permute-start.11 = (f32[640,128]{1,0:T(8,128)}, f32[640,128]{1,0:T(8,128)S(1)}, u32[]{:S(2)}, u32[]{:S(2)}) collective-permute-start(f32[640,128]{1,0:T(8,128)} %shard_map.21.own_ref), channel_id=1, source_target_pairs={{0,2},{1,3},{2,0},{3,1},{4,6},{5,7},{6,4},{7,5},{8,10},{9,11},{10,... | collective-permute-start | bytes 983048 | tf_op jit(solution)/shard_map/ppermute | solution.py:406
  162.1 63.3 %collective-permute-start.10 = (bf16[2,2,152,256]{3,2,1,0:T(8,128)(2,1)}, bf16[2,2,152,256]{3,2,1,0:T(8,128)(2,1)S(1)}, u32[]{:S(2)}, u32[]{:S(2)}) collective-permute-start(bf16[2,2,152,256]{3,2,1,0:T(8,128)(2,1)} %pad_maximum_fusion.refs_2_), channel_id=1, source_target_pairs={{0,3},{1,2},{2,1},{3,0},{4,7},{5,6},{6,5},{7,4},{8,11},{9,10},{10,... | collective-permute-start | bytes 933896 | tf_op jit(solution)/shard_map/ppermute | solution.py:406
  164.0 76.0 %collective-permute-start.8 = (bf16[2,2,152,256]{3,2,1,0:T(8,128)(2,1)}, bf16[2,2,152,256]{3,2,1,0:T(8,128)(2,1)S(1)}, u32[]{:S(2)}, u32[]{:S(2)}) collective-permute-start(bf16[2,2,152,256]{3,2,1,0:T(8,128)(2,1)} %pad_maximum_fusion.refs_2_), channel_id=1, source_target_pairs={{0,2},{1,3},{2,0},{3,1},{4,6},{5,7},{6,4},{7,5},{8,10},{9,11},{10,... | collective-permute-start | bytes 933896 | tf_op jit(solution)/shard_map/ppermute | solution.py:406
  225.4 0.7 copy-start.6
  240.0 46.8 %copy-start.1 = (f32[640,128]{1,0:T(8,128)S(1)}, f32[640,128]{1,0:T(8,128)}, u32[]{:S(2)}) copy-start(f32[640,128]{1,0:T(8,128)} %shard_map.21.own_ref) | copy-start | bytes 983044
  240.0 0.7 copy-start.5
  254.6 0.7 copy-start.2
  269.8 10.5 %all-to-all-start.7 = ((f32[8,16,128]{2,1,0:T(8,128)}), f32[8,16,128]{2,1,0:T(8,128)S(1)}, u32[]{:S(2)}, u32[]{:S(2)}) async-start(f32[8,16,128]{2,1,0:T(8,128)} %broadcast_in_dim.16), calls=%async_computation.7 | async-start | bytes 131072 | tf_op jit(solution)/shard_map/all_to_all | solution.py:418
  281.0 26.1 %all-to-all-start.8 = ((f32[8,16,128]{2,1,0:T(8,128)}), f32[8,16,128]{2,1,0:T(8,128)S(1)}, u32[]{:S(2)}, u32[]{:S(2)}) async-start(f32[8,16,128]{2,1,0:T(8,128)} %broadcast_in_dim.17), calls=%async_computation.8 | async-start | bytes 131072 | tf_op jit(solution)/shard_map/all_to_all | solution.py:418
  287.5 9.4 %copy-start.3 = (f32[640,128]{1,0:T(8,128)S(1)}, f32[640,128]{1,0:T(8,128)}, u32[]{:S(2)}) copy-start(f32[640,128]{1,0:T(8,128)} %copy-done.2) | copy-start | bytes 983044
  307.1 0.6 copy-start.7
